TPU v7x, 128 devices: a whole 4x4x4 slice. The times are simulated.
128 devices in a mesh: wide: 8 (over y_lo, z), narrow: 16 (over y_hi, x, core).
Axes of the slice: x: 4, y: 4 (y_hi: 2, y_lo: 2; y = y_hi * 2 + y_lo), z: 4, core: 2. Of those that a mesh axis runs over, the one named last changes fastest.
Arguments:
- hidden: bfloat16 [1024, 4096], P('wide', 'narrow'), may hold values from -6 to 6
- norm_gain: float32 [4096], replicated, may hold values from 0.1 to 1.9
- w_query: bfloat16 [4096, 8192], P(None, 'narrow'), may hold values from -0.09375 to 0.09375
- w_keyval: bfloat16 [4096, 1024], P('narrow'), may hold values from -0.09375 to 0.09375
- query_gain: float32 [128], replicated, may hold values from 0.5 to 4
- key_gain: float32 [128], replicated, may hold values from 0.5 to 4
- cache_keys: bfloat16 [64, 16384, 512], P('wide', 'narrow'), may hold values from -300 to 300
- cache_values: bfloat16 [64, 16384, 512], P('wide', 'narrow'), may hold values from -6 to 6
- cache_lengths: int32 [64], P('wide'), may hold values from 1 to 16384
- owner_rank: int32 [64], P('wide'), may hold values from 0 to 7, as said below
- draft_mask: int32 [64, 16, 16], P('wide'), may hold values from 0 to 1, as said below
- w_output: bfloat16 [8192, 4096], P('narrow'), may hold values from -0.0625 to 0.0625
Outputs:
- projected: bfloat16 [1024, 4096], P('wide', 'narrow')
Inputs may be any that keep to these rules, and one draw needn't show every extreme that they name: `owner_rank`: in each aligned block of 8 requests every index of wide is named exactly 1 times. Row t of a request marks the ancestors of draft token t in a tree of draft tokens and t itself: draft_mask[r, t, t] = 1 and draft_mask[r, t, u] = 0 for u > t.
All inputs are finite; a program needn't handle non-finite values.
Results may differ from a plain program's by a relative error of at most 0.007.
The roundings to bfloat16 on the way count: a program that leaves them out, or rounds other values in their place, can miss the bound.
Values may be sent and summed in bfloat16 or wider, within the bound.
No kernel may reach another device: no remote copies, remote signals or barrier semaphores. Data moves between devices by JAX's collectives and lax.ppermute only.
A program may use at most 192 MiB of HBM per device.

v0:
```python
import functools
import math

import jax
import jax.numpy as jnp
from jax import lax
from jax.experimental import pallas as pl
from jax.experimental.pallas import tpu as pltpu
from jax.sharding import Mesh
from jax.sharding import PartitionSpec as P

HQ = 64
KVH = 4
HD = 128
DRAFT = 16
WIDE = 8
CHIPS = 8
CORES = 2
PER_HEAD = HQ // (CHIPS * CORES)
ROWS = PER_HEAD * DRAFT

EPS = 1e-06
DEAD = -1e30
LOG2E = 1.4426950408889634
SCALE2 = LOG2E / math.sqrt(HD)
F32 = jnp.float32
BF16 = jnp.bfloat16


def vmem():
    return pl.BlockSpec(memory_space=pltpu.VMEM)


def smem():
    return pl.BlockSpec(memory_space=pltpu.SMEM)


def anywhere():
    return pl.BlockSpec(memory_space=pl.ANY)


def rms(values, gain_row):
    mean = jnp.mean(values * values, axis=-1, keepdims=True)
    return values * lax.rsqrt(mean + EPS) * gain_row


def route_kernel(owner_ref, hidden_ref, mask_ref, out_ref):
    blank = jnp.zeros((DRAFT // 2, HD - 2 * DRAFT), F32)
    for r in range(WIDE):
        target = owner_ref[r]
        low = hidden_ref[r * DRAFT : (r + 1) * DRAFT, :HD]
        high = hidden_ref[r * DRAFT : (r + 1) * DRAFT, HD:]
        marks = mask_ref[r].astype(F32)
        marks = jnp.concatenate([marks[: DRAFT // 2], marks[DRAFT // 2 :], blank], axis=1)
        marks = marks.astype(BF16)
        for c in range(CHIPS):
            out_ref[target, c, 0:16, :] = low
            out_ref[target, c, 16:32, :] = high
            out_ref[target, c, 32:40, :] = marks


def features(ref, c):
    low = ref[:, c, 0:16, :].reshape(WIDE * DRAFT, HD)
    high = ref[:, c, 16:32, :].reshape(WIDE * DRAFT, HD)
    return jnp.concatenate([low, high], axis=1)


def query_kernel(
    own_ref,
    other_ref,
    gain_far,
    wq_far,
    wkv_far,
    qgain_far,
    out_ref,
    kv_ref,
    mine_ref,
    marks_ref,
    gain_ref,
    wq_ref,
    wkv_ref,
    qgain_ref,
    sem,
):
    gain_copy = pltpu.make_async_copy(gain_far, gain_ref, sem.at[0])
    qgain_copy = pltpu.make_async_copy(qgain_far, qgain_ref, sem.at[1])
    wkv_copy = pltpu.make_async_copy(wkv_far, wkv_ref, sem.at[2])
    wq_copies = [
        pltpu.make_async_copy(wq_far.at[c], wq_ref.at[c], sem.at[3 + c]) for c in range(CHIPS)
    ]
    for copy in [gain_copy, qgain_copy] + wq_copies + [wkv_copy]:
        copy.start()
    core = lax.axis_index("core")
    chip = lax.axis_index("chip")
    tokens = WIDE * DRAFT
    squares = jnp.zeros((tokens, 2 * HD), F32)
    for ref in (own_ref, other_ref):
        for c in range(CHIPS):
            block = features(ref, c).astype(F32)
            squares = squares + block * block
    width = CHIPS * CORES * 2 * HD
    scale = lax.rsqrt(jnp.sum(squares, axis=-1, keepdims=True) * (1.0 / width) + EPS)

    def normed(ref, c, side):
        block = features(ref, c).astype(F32)
        gain = gain_ref[pl.ds((c * CORES + side) * 2, 2), :]
        gain = jnp.concatenate([gain[0:1], gain[1:2]], axis=1)
        return (block * scale * gain).astype(BF16)

    gain_copy.wait()
    total = jnp.zeros((tokens, PER_HEAD * HD), F32)
    for c in range(CHIPS):
        wq_copies[c].wait()
        for ref, side in ((own_ref, core), (other_ref, 1 - core)):
            total = total + jnp.dot(
                normed(ref, c, side), wq_ref[c, side], preferred_element_type=F32
            )
    qgain_copy.wait()
    for j in range(PER_HEAD):
        head = rms(total[:, j * HD : (j + 1) * HD], qgain_ref[...]).astype(BF16)
        head = head.reshape(WIDE, DRAFT, HD)
        for b in range(WIDE):
            start = b * ROWS + j * DRAFT
            mine_ref[start : start + DRAFT, :] = head[b]
            for c in range(CHIPS):
                out_ref[c, start : start + DRAFT, :] = head[b]
    for b in range(WIDE):
        marks_ref[b] = own_ref[b, 0, 32:40, :]
    wkv_copy.wait()
    keyval = jnp.dot(normed(own_ref, chip, core), wkv_ref[...], preferred_element_type=F32)
    for c in range(CHIPS):
        kv = c // (CHIPS // KVH)
        keys = keyval[:, kv * HD : (kv + 1) * HD]
        values = keyval[:, (KVH + kv) * HD : (KVH + kv + 1) * HD]
        kv_ref[c, 0:tokens, :] = keys.astype(BF16)
        kv_ref[c, tokens : 2 * tokens, :] = values.astype(BF16)


def attend_kernel(
    first, length_ref, q_own_ref, q_other_ref, key_ref, value_ref, o_own_ref, o_other_ref, lse_ref,
    s_ref, p_ref, m_ref,
):
    b = pl.program_id(0)
    span = key_ref.shape[1]
    tile = 2 * HD
    tiles = span // tile
    index = lax.axis_index("chip") * CORES + lax.axis_index("core")
    live = length_ref[first + b] - index * span
    ones = jnp.ones((span, HD), BF16)
    rows = lax.broadcasted_iota(jnp.int32, (HD, HD), 0)
    lanes = lax.broadcasted_iota(jnp.int32, (HD, HD), 1)

    def query(kv):
        return jnp.concatenate(
            [q_own_ref[2 * kv], q_own_ref[2 * kv + 1], q_other_ref[2 * kv], q_other_ref[2 * kv + 1]],
            axis=0,
        )

    def score(kv, i, q, top, masked):
        at = slice(i * tile, (i + 1) * tile)
        keys = key_ref[0, at, kv * HD : (kv + 1) * HD]
        part = lax.dot_general(q, keys, (((1,), (1,)), ((), ())), preferred_element_type=F32)
        if masked:
            place = lax.broadcasted_iota(jnp.int32, (1, tile), 1) + i * tile
            part = jnp.where(place < live, part, DEAD)
        s_ref[kv % 2, :, at] = part
        high = jnp.maximum(part[:, :HD], part[:, HD:])
        return high if top is None else jnp.maximum(top, high)

    def close(kv, top):
        m_ref[kv % 2] = jnp.broadcast_to(jnp.max(top, axis=-1, keepdims=True), top.shape)

    def soft(kv, i):
        count = KVH * ROWS // tiles
        at = slice(i * count, (i + 1) * count)
        top = m_ref[kv % 2, at, :]
        for j in range(span // HD):
            part = s_ref[kv % 2, at, j * HD : (j + 1) * HD]
            p_ref[kv % 2, at, j * HD : (j + 1) * HD] = jnp.exp2((part - top) * SCALE2).astype(BF16)

    def value(kv):
        values = jnp.concatenate([value_ref[0, :, kv * HD : (kv + 1) * HD], ones], axis=1)
        summed = jnp.dot(p_ref[kv % 2], values, preferred_element_type=F32)
        den = summed[:, HD:]
        out = (summed[:, :HD] / den).astype(BF16)
        o_own_ref[2 * kv] = out[0 * ROWS : 1 * ROWS]
        o_own_ref[2 * kv + 1] = out[1 * ROWS : 2 * ROWS]
        o_other_ref[2 * kv] = out[2 * ROWS : 3 * ROWS]
        o_other_ref[2 * kv + 1] = out[3 * ROWS : 4 * ROWS]
        lse = m_ref[kv % 2] * SCALE2 + jnp.log2(den)
        for side in range(2):
            block = lse[side * HD : (side + 1) * HD]
            line = jnp.sum(jnp.where(rows == lanes, block, 0.0), axis=0, keepdims=True)
            lse_ref[0, side * KVH + kv : side * KVH + kv + 1, :] = line

    def whole(masked):
        for stage in range(KVH + 1):
            top = None
            q = query(stage) if stage < KVH else None
            for i in range(tiles):
                if stage < KVH:
                    top = score(stage, i, q, top, masked)
                if stage > 0:
                    soft(stage - 1, i)
            if stage > 0:
                value(stage - 1)
            if stage < KVH:
                close(stage, top)

    @pl.when(live <= 0)
    def _():
        o_own_ref[...] = jnp.zeros(o_own_ref.shape, BF16)
        o_other_ref[...] = jnp.zeros(o_other_ref.shape, BF16)
        lse_ref[...] = jnp.full(lse_ref.shape, DEAD, F32)

    @pl.when(live >= span)
    def _():
        whole(False)

    @pl.when(jnp.logical_and(live > 0, live < span))
    def _():
        whole(True)


def join_kernel(
    mine_ref, theirs_ref, lse_ref, lse_in_ref, kv_own_ref, kv_other_ref, out_ref, kv_ref
):
    one = lse_ref[:, 0:KVH, :].reshape(WIDE * KVH, HD)
    two = lse_in_ref[:, KVH : 2 * KVH, :].reshape(WIDE * KVH, HD)
    top = jnp.maximum(one, two)
    weight_one = jnp.exp2(one - top)
    weight_two = jnp.exp2(two - top)
    den = weight_one + weight_two
    lse = (top + jnp.log2(den)).reshape(WIDE, KVH, HD)
    shares = jnp.concatenate(
        [weight_one / den, weight_two / den, jnp.zeros((2 * WIDE * KVH, HD), F32)], axis=0
    )
    shares = shares.T
    for b in range(WIDE):
        for kv in range(KVH):
            j = b * KVH + kv
            col_one = shares[:, j : j + 1]
            col_two = shares[:, WIDE * KVH + j : WIDE * KVH + j + 1]
            for p in range(2):
                c = 2 * kv + p
                at = slice(b * ROWS, (b + 1) * ROWS)
                part = slice(p * ROWS, (p + 1) * ROWS)
                mixed = (
                    mine_ref[c, at, :].astype(F32) * col_one[part]
                    + theirs_ref[c, at, :].astype(F32) * col_two[part]
                )
                out_ref[c, at, :] = mixed.astype(BF16)
    lanes = lax.broadcasted_iota(jnp.int32, (WIDE, HD), 1)
    for kv in range(KVH):
        line = lse[:, kv, :]
        first = line.astype(BF16).astype(F32)
        rest = line - first
        second = rest.astype(BF16).astype(F32)
        third = (rest - second).astype(BF16).astype(F32)
        turned = [pltpu.roll(x, ROWS, 1) for x in (first, second, third)]
        for p in range(2):
            a = first if p == 0 else turned[0]
            m = turned[1] if p == 0 else second
            z = third if p == 0 else turned[2]
            base = WIDE * ROWS
            tail = jnp.concatenate(
                [jnp.where(lanes < ROWS, a, m), jnp.where(lanes < ROWS, z, 0.0)], axis=0
            )
            out_ref[2 * kv + p, base : base + 2 * WIDE, :] = tail.astype(BF16)
    total = jnp.zeros(kv_ref.shape, F32)
    for ref in (kv_own_ref, kv_other_ref):
        for c in range(CHIPS):
            total = total + ref[c].astype(F32)
    kv_ref[...] = total


def draft_kernel(q_ref, kv_ref, kgain_ref, mask_ref, out_ref, lse_ref):
    tokens = WIDE * DRAFT
    keys = rms(kv_ref[0:tokens, :], kgain_ref[...]).astype(BF16)
    values = kv_ref[tokens : 2 * tokens, :].astype(BF16)
    lanes = lax.broadcasted_iota(jnp.int32, (DRAFT, HD), 1)
    for b in range(WIDE):
        at = slice(b * ROWS, (b + 1) * ROWS)
        marks = mask_ref[b].astype(F32)
        late = pltpu.roll(marks, HD - DRAFT, 1)
        marks = jnp.concatenate([marks, late], axis=0)
        marks = jnp.where(lanes < DRAFT, marks, 0.0)
        if b:
            marks = pltpu.roll(marks, b * DRAFT, 1)
        allowed = jnp.concatenate([marks] * PER_HEAD, axis=0) > 0.5
        scores = lax.dot_general(
            q_ref[at, :], keys, (((1,), (1,)), ((), ())), preferred_element_type=F32
        )
        scores = jnp.where(allowed, scores, DEAD)
        top = jnp.max(scores, axis=-1, keepdims=True)
        weights = jnp.exp2((scores - top) * SCALE2)
        den = jnp.sum(weights, axis=-1, keepdims=True)
        summed = jnp.dot(weights.astype(BF16), values, preferred_element_type=F32)
        out_ref[at, :] = summed / den
        lse_ref[at, :] = jnp.broadcast_to(top * SCALE2 + jnp.log2(den), (ROWS, HD))


def finish_kernel(
    part_ref, draft_ref, lse_ref, wo_far, out_own_ref, out_other_ref, wo_ref, sem
):
    core = lax.axis_index("core")
    tokens = WIDE * DRAFT
    wo_copies = []
    for c in range(CHIPS):
        columns = pl.ds(c * CORES * 2 * HD, CORES * 2 * HD)
        wo_copies.append(
            pltpu.make_async_copy(wo_far.at[:, columns], wo_ref.at[:, columns], sem.at[c])
        )
        wo_copies[c].start()
    base = WIDE * ROWS
    lines = []
    for c in range(CHIPS):
        head = part_ref[c, base : base + WIDE, :].astype(F32)
        tail = part_ref[c, base + WIDE : base + 2 * WIDE, :].astype(F32)
        lines.append(head + pltpu.roll(head, ROWS, 1) + tail)
    columns = jnp.concatenate(lines + [jnp.zeros((HD - CHIPS * WIDE, HD), F32)], axis=0).T
    attended = []
    for b in range(WIDE):
        at = slice(b * ROWS, (b + 1) * ROWS)
        cols = [columns[0:ROWS, c * WIDE + b : c * WIDE + b + 1] for c in range(CHIPS)]
        cols = [jnp.broadcast_to(col, (ROWS, HD)) for col in cols]
        draft = lse_ref[at, :]
        peak = draft
        for col in cols:
            peak = jnp.maximum(peak, col)
        share = jnp.exp2(draft - peak)
        numer = draft_ref[at, :] * share
        denom = share
        for c in range(CHIPS):
            share = jnp.exp2(cols[c] - peak)
            numer = numer + part_ref[c, at, :].astype(F32) * share
            denom = denom + share
        attended.append((numer / denom).astype(BF16))
    attended = jnp.stack(attended, axis=0)
    rows = jnp.concatenate(
        [
            attended[:, j * DRAFT : (j + 1) * DRAFT, :].reshape(tokens, HD)
            for j in range(PER_HEAD)
        ],
        axis=1,
    )
    piece = 2 * HD
    for c in range(CHIPS):
        wo_copies[c].wait()
        for ref, side in ((out_own_ref, core), (out_other_ref, 1 - core)):
            column = pl.multiple_of((c * CORES + side) * piece, piece)
            out = jnp.dot(rows, wo_ref[:, pl.ds(column, piece)], preferred_element_type=F32)
            ref[:, c] = out.astype(BF16).reshape(WIDE, DRAFT, piece)


def pair_kernel(one_ref, two_ref, out_ref):
    out_ref[...] = (one_ref[...].astype(F32) + two_ref[...].astype(F32)).astype(BF16)


def gather_kernel(owner_ref, part_ref, out_ref):
    for r in range(WIDE):
        source = owner_ref[r]
        total = part_ref[source, 0].astype(F32)
        for c in range(1, CHIPS):
            total = total + part_ref[source, c].astype(F32)
        out_ref[r * DRAFT : (r + 1) * DRAFT, :] = total.astype(BF16)


def swap(x):
    return lax.ppermute(x, "core", [(0, 1), (1, 0)])


def exchange(x, axes):
    return lax.all_to_all(x, axes, split_axis=0, concat_axis=0, tiled=True)


def local(
    hidden,
    norm_gain,
    w_query,
    w_keyval,
    query_gain,
    key_gain,
    cache_keys,
    cache_values,
    cache_lengths,
    owner_rank,
    draft_mask,
    w_output,
):
    tokens = WIDE * DRAFT
    piece = 2 * HD
    span = cache_keys.shape[1]
    shape = jax.ShapeDtypeStruct

    far = lambda x: pltpu.with_memory_space_constraint(x, pltpu.HBM)
    sent = pl.pallas_call(
        route_kernel,
        compiler_params=pltpu.CompilerParams(vmem_limit_bytes=4 * 1024 * 1024),
        out_shape=shape((WIDE, CHIPS, 40, HD), BF16),
        in_specs=[smem(), vmem(), vmem()],
        out_specs=vmem(),
    )(far(owner_rank), far(hidden), far(draft_mask))
    arrived = exchange(sent.reshape(WIDE * CHIPS, 40, HD), ("wide", "chip"))
    partner = swap(arrived)
    arrived = arrived.reshape(WIDE, CHIPS, 40, HD)
    partner = partner.reshape(WIDE, CHIPS, 40, HD)

    queries, keyval, mine, marks = pl.pallas_call(
        query_kernel,
        compiler_params=pltpu.CompilerParams(vmem_limit_bytes=16 * 1024 * 1024),
        out_shape=(
            shape((CHIPS, WIDE * ROWS, HD), BF16),
            shape((CHIPS, 2 * tokens, HD), BF16),
            shape((WIDE * ROWS, HD), BF16),
            shape((WIDE, DRAFT // 2, HD), BF16),
        ),
        in_specs=[vmem()] * 2 + [anywhere()] * 4,
        out_specs=(vmem(),) * 4,
        scratch_shapes=[
            pltpu.VMEM((CHIPS * CORES * 2, HD), F32),
            pltpu.VMEM((CHIPS, CORES, piece, PER_HEAD * HD), BF16),
            pltpu.VMEM((piece, 2 * KVH * HD), BF16),
            pltpu.VMEM((1, HD), F32),
            pltpu.SemaphoreType.DMA((3 + CHIPS,)),
        ],
    )(
        arrived,
        partner,
        far(norm_gain.reshape(CHIPS * CORES * 2, HD)),
        far(w_query.reshape(CHIPS, CORES, piece, PER_HEAD * HD)),
        far(w_keyval),
        far(query_gain.reshape(1, HD)),
    )
    q_own = exchange(queries, "chip")
    q_own, keyval = lax.optimization_barrier((q_own, keyval))
    kv_own = exchange(keyval, "chip")
    q_other = swap(q_own)

    q_spec = pl.BlockSpec((CHIPS, ROWS, HD), lambda b: (0, b, 0))
    kv_spec = pl.BlockSpec((1, span, KVH * HD), lambda b: (b, 0, 0))
    attend = pl.pallas_call(
        functools.partial(attend_kernel, 0),
        cost_estimate=pl.CostEstimate(
            flops=8 * WIDE * KVH * KVH * ROWS * span * HD,
            bytes_accessed=4 * WIDE * span * KVH * HD,
            transcendentals=WIDE * KVH * KVH * ROWS * span,
        ),
        compiler_params=pltpu.CompilerParams(vmem_limit_bytes=16 * 1024 * 1024),
        scratch_shapes=[
            pltpu.VMEM((2, KVH * ROWS, span), F32),
            pltpu.VMEM((2, KVH * ROWS, span), BF16),
            pltpu.VMEM((2, KVH * ROWS, HD), F32),
        ],
        out_shape=(
            shape((CHIPS, WIDE * ROWS, HD), BF16),
            shape((CHIPS, WIDE * ROWS, HD), BF16),
            shape((WIDE, 2 * KVH, HD), F32),
        ),
        grid=(WIDE,),
        in_specs=[smem(), q_spec, q_spec, kv_spec, kv_spec],
        out_specs=(q_spec, q_spec, pl.BlockSpec((1, 2 * KVH, HD), lambda b: (b, 0, 0))),
    )
    o_own, o_other, lse = attend(
        cache_lengths, q_own, far(q_other), far(cache_keys), far(cache_values)
    )

    kv_other = swap(kv_own)
    joined, keyval = pl.pallas_call(
        join_kernel,
        compiler_params=pltpu.CompilerParams(vmem_limit_bytes=8 * 1024 * 1024),
        out_shape=(
            shape((CHIPS, WIDE * ROWS + 2 * WIDE, HD), BF16),
            shape((2 * tokens, HD), F32),
        ),
        in_specs=[vmem()] * 6,
        out_specs=(vmem(), vmem()),
    )(o_own, swap(o_other), lse, swap(lse), kv_own, kv_other)
    parts = exchange(joined, "chip")

    drafted, draft_lse = pl.pallas_call(
        draft_kernel,
        compiler_params=pltpu.CompilerParams(vmem_limit_bytes=8 * 1024 * 1024),
        cost_estimate=pl.CostEstimate(
            flops=4000000000, bytes_accessed=2000000, transcendentals=70000
        ),
        out_shape=(shape((WIDE * ROWS, HD), F32),) * 2,
        in_specs=[vmem()] * 4,
        out_specs=(vmem(), vmem()),
    )(mine, keyval, key_gain.reshape(1, HD), marks)

    out_own, out_other = pl.pallas_call(
        finish_kernel,
        compiler_params=pltpu.CompilerParams(vmem_limit_bytes=16 * 1024 * 1024),
        out_shape=(shape((WIDE, CHIPS, DRAFT, piece), BF16),) * 2,
        in_specs=[vmem()] * 3 + [anywhere()],
        out_specs=(vmem(), vmem()),
        scratch_shapes=[
            pltpu.VMEM(w_output.shape, BF16),
            pltpu.SemaphoreType.DMA((CHIPS,)),
        ],
    )(parts, drafted, draft_lse, far(w_output))

    summed = pl.pallas_call(
        pair_kernel,
        compiler_params=pltpu.CompilerParams(vmem_limit_bytes=4 * 1024 * 1024),
        out_shape=shape((WIDE, CHIPS, DRAFT, piece), BF16),
        in_specs=[vmem()] * 2,
        out_specs=vmem(),
    )(out_own, swap(out_other))
    back = exchange(summed.reshape(WIDE * CHIPS, DRAFT, piece), ("wide", "chip"))
    return pl.pallas_call(
        gather_kernel,
        compiler_params=pltpu.CompilerParams(vmem_limit_bytes=4 * 1024 * 1024),
        out_shape=shape((tokens, piece), BF16),
        in_specs=[smem(), vmem()],
        out_specs=vmem(),
    )(owner_rank, back.reshape(WIDE, CHIPS, DRAFT, piece))


def solution(mesh):
    fine = Mesh(mesh.devices.reshape(WIDE, CHIPS, CORES), ("wide", "chip", "core"))
    narrow = ("chip", "core")
    in_specs = (
        P("wide", narrow),
        P(),
        P(None, narrow),
        P(narrow, None),
        P(),
        P(),
        P("wide", narrow, None),
        P("wide", narrow, None),
        P("wide"),
        P("wide"),
        P("wide", None, None),
        P(narrow, None),
    )
    out_specs = P("wide", narrow)

    return jax.shard_map(local, mesh=fine, in_specs=in_specs, out_specs=out_specs, check_vma=False)
```

profile of v0, /device:TPU:0, one launch (start us, length us, event | category | flops | bytes accessed | tf_op | source)
XLA Modules:
  0.0 137.1 jit_solution(15187136453993449151)
XLA Ops:
  0.0 1.0 shard_map.118
  1.0 25.6 %all_to_all.25 = bf16[64,40,128]{2,1,0:T(8,128)(2,1)S(1)} all-to-all(bf16[64,40,128]{2,1,0:T(8,128)(2,1)S(1)} %bitcast.10), channel_id=1, replica_groups=mesh['wide'=8,'chip'=8,'core'=2] {'wide','chip'}, dimensions={0} | all-to-all | bytes 1310720 | tf_op jit(solution)/shard_map/all_to_all | solution.py:374
  26.6 0.0 copy-start.1
  26.6 0.0 collective-permute-start
  26.6 2.1 %collective-permute-done = bf16[64,40,128]{2,1,0:T(8,128)(2,1)S(1)} collective-permute-done((bf16[64,40,128]{2,1,0:T(8,128)(2,1)S(1)}, bf16[64,40,128]{2,1,0:T(8,128)(2,1)S(1)}, u32[]{:S(2)}, u32[]{:S(2)}) %collective-permute-start) | collective-permute-done | bytes 655392 | tf_op jit(solution)/shard_map/ppermute | solution.py:370
  28.7 3.0 %shard_map.119 = (bf16[8,512,128]{2,1,0:T(8,128)(2,1)S(1)}, bf16[8,256,128]{2,1,0:T(8,128)(2,1)S(1)}, bf16[512,128]{1,0:T(8,128)(2,1)S(1)}, bf16[8,8,128]{2,1,0:T(8,128)(2,1)S(1)}) custom-call(bf16[8,8,40,128]{3,2,1,0:T(8,128)(2,1)S(1)} %bitcast.9, bf16[8,8,40,128]{3,2,1,0:T(8,128)(2,1)S(1)} %bitcast.13, f32[32,128]{1,0:T(8,128)} %bitcast.16, ...), custom_call_target="tpu_custom_call" | custom-call | tf_op jit(solution)/shard_map/pallas_call | solution.py:409
  31.7 20.9 %all_to_all.26.q_own_ref = bf16[8,512,128]{2,1,0:T(8,128)(2,1)S(1)} all-to-all(bf16[8,512,128]{2,1,0:T(8,128)(2,1)S(1)} %get-tuple-element.20), channel_id=1, replica_groups=mesh['wide'=8,'chip'=8,'core'=2] {'chip'}, dimensions={0} | all-to-all | bytes 2097152 | tf_op jit(solution)/shard_map/all_to_all | solution.py:374
  52.6 0.0 collective-permute-start.1
  52.6 2.7 %collective-permute-done.1.q_other_ref = bf16[8,512,128]{2,1,0:T(8,128)(2,1)S(1)} collective-permute-done((bf16[8,512,128]{2,1,0:T(8,128)(2,1)S(1)}, bf16[8,512,128]{2,1,0:T(8,128)(2,1)S(1)}, u32[]{:S(2)}, u32[]{:S(2)}) %collective-permute-start.1) | collective-permute-done | bytes 1048608 | tf_op jit(solution)/shard_map/ppermute | solution.py:370
  55.3 0.0 copy-start.3
  55.3 1.0 copy-done.3
  56.2 0.0 copy-done.1
  56.2 15.4 %shard_map.120 = (bf16[8,512,128]{2,1,0:T(8,128)(2,1)S(1)}, bf16[8,512,128]{2,1,0:T(8,128)(2,1)S(1)}, f32[8,8,128]{2,1,0:T(8,128)S(1)}) custom-call(s32[8]{0:T(128)S(1)} %copy-done.1, bf16[8,512,128]{2,1,0:T(8,128)(2,1)S(1)} %all_to_all.26.q_own_ref, bf16[8,512,128]{2,1,0:T(8,128)(2,1)} %copy-done.3, bf16[8,1024,512]{2,1,0:T(8,128)(2,1)} %key_ref.1, ...), custom_call_target="tpu_custom_call" | custom-call | flops 8589934592 | bytes 16777216 | tf_op jit(solution)/shard_map/pallas_call | solution.py:464
  71.7 0.0 copy-start.2
  71.7 0.1 collective-permute-start.2
  71.8 14.9 %all_to_all.27.kv_own_ref = bf16[8,256,128]{2,1,0:T(8,128)(2,1)S(1)} all-to-all(bf16[8,256,128]{2,1,0:T(8,128)(2,1)S(1)} %get-tuple-element.26), channel_id=1, replica_groups=mesh['wide'=8,'chip'=8,'core'=2] {'chip'}, dimensions={0} | all-to-all | bytes 1048576 | tf_op jit(solution)/shard_map/all_to_all | solution.py:374
  86.7 0.0 collective-permute-start.4
  86.7 0.5 collective-permute-start.3
  87.2 1.4 %collective-permute-done.4.kv_other_ref = bf16[8,256,128]{2,1,0:T(8,128)(2,1)S(1)} collective-permute-done((bf16[8,256,128]{2,1,0:T(8,128)(2,1)S(1)}, bf16[8,256,128]{2,1,0:T(8,128)(2,1)S(1)}, u32[]{:S(2)}, u32[]{:S(2)}) %collective-permute-start.4) | collective-permute-done | bytes 524320 | tf_op jit(solution)/shard_map/ppermute | solution.py:370
  88.6 0.0 collective-permute-done.3.lse_in_ref
  88.7 0.0 collective-permute-done.2.theirs_ref
  88.7 2.5 %shard_map.121 = (bf16[8,528,128]{2,1,0:T(8,128)(2,1)}, f32[256,128]{1,0:T(8,128)S(1)}) custom-call(bf16[8,512,128]{2,1,0:T(8,128)(2,1)S(1)} %get-tuple-element.23.mine_ref, bf16[8,512,128]{2,1,0:T(8,128)(2,1)S(1)} %collective-permute-done.2.theirs_ref, f32[8,8,128]{2,1,0:T(8,128)S(1)} %get-tuple-element.25.lse_ref, ...), custom_call_target="tpu_custom_call" | custom-call | tf_op jit(solution)/shard_map/pallas_call | solution.py:469
  91.2 3.6 %all-to-all-start.3 = ((bf16[8,528,128]{2,1,0:T(8,128)(2,1)}), bf16[8,528,128]{2,1,0:T(8,128)(2,1)S(1)}, u32[]{:S(2)}, u32[]{:S(2)}) async-start(bf16[8,528,128]{2,1,0:T(8,128)(2,1)} %get-tuple-element.27), calls=%async_computation.3 | async-start | bytes 2162688 | tf_op jit(solution)/shard_map/all_to_all | solution.py:374
  94.8 0.0 copy-done.2
  94.8 2.1 %shard_map.122 = (f32[512,128]{1,0:T(8,128)S(1)}, f32[512,128]{1,0:T(8,128)S(1)}) custom-call(bf16[512,128]{1,0:T(8,128)(2,1)S(1)} %get-tuple-element.28.q_ref, f32[256,128]{1,0:T(8,128)S(1)} %get-tuple-element.29.kv_ref, f32[1,128]{1,0:T(1,128)S(1)} %bitcast.14, bf16[8,8,128]{2,1,0:T(8,128)(2,1)S(1)} %get-tuple-element.30.mask_ref), custom_call_target="tpu_custom_call" | custom-call | flops 4000000000 | bytes 2000000 | tf_op jit(solution)/shard_map/pallas_call | solution.py:481
  96.9 16.0 %all-to-all-done.3.part_ref = bf16[8,528,128]{2,1,0:T(8,128)(2,1)S(1)} async-done(((bf16[8,528,128]{2,1,0:T(8,128)(2,1)}), bf16[8,528,128]{2,1,0:T(8,128)(2,1)S(1)}, u32[]{:S(2)}, u32[]{:S(2)}) %all-to-all-start.3) | async-done | bytes 1081376 | tf_op jit(solution)/shard_map/all_to_all | solution.py:374
  112.8 0.0 copy-start
  112.8 3.1 %shard_map.123 = (bf16[8,8,16,256]{3,2,1,0:T(8,128)(2,1)S(1)}, bf16[8,8,16,256]{3,2,1,0:T(8,128)(2,1)S(1)}) custom-call(bf16[8,528,128]{2,1,0:T(8,128)(2,1)S(1)} %all-to-all-done.3.part_ref, f32[512,128]{1,0:T(8,128)S(1)} %get-tuple-element.31.draft_ref, f32[512,128]{1,0:T(8,128)S(1)} %get-tuple-element.32.lse_ref, bf16[512,4096]{1,0:T(8,128)(2,1)} %wo_far.1), custom_call_target="tpu_custom_call" | custom-call | tf_op jit(solution)/shard_map/pallas_call | solution.py:492
  115.9 0.1 collective-permute-start.5
  116.0 1.9 %collective-permute-done.5.two_ref = bf16[8,8,16,256]{3,2,1,0:T(8,128)(2,1)S(1)} collective-permute-done((bf16[8,8,16,256]{3,2,1,0:T(8,128)(2,1)S(1)}, bf16[8,8,16,256]{3,2,1,0:T(8,128)(2,1)S(1)}, u32[]{:S(2)}, u32[]{:S(2)}) %collective-permute-start.5) | collective-permute-done | bytes 524320 | tf_op jit(solution)/shard_map/ppermute | solution.py:370
  117.9 0.1 shard_map.124
  118.0 17.8 %all_to_all.28 = bf16[64,16,256]{2,1,0:T(8,128)(2,1)S(1)} all-to-all(bf16[64,16,256]{2,1,0:T(8,128)(2,1)S(1)} %bitcast.11), channel_id=1, replica_groups=mesh['wide'=8,'chip'=8,'core'=2] {'wide','chip'}, dimensions={0} | all-to-all | bytes 1048576 | tf_op jit(solution)/shard_map/all_to_all | solution.py:374
  135.8 0.0 copy-done
  135.8 1.2 shard_map.125
Async XLA Ops:
  26.6 29.6 %copy-start.1 = (s32[8]{0:T(128)S(1)}, s32[8]{0:T(128)}, u32[]{:S(2)}) copy-start(s32[8]{0:T(128)} %length_ref.1) | copy-start | bytes 100
  26.6 2.1 %collective-permute-start = (bf16[64,40,128]{2,1,0:T(8,128)(2,1)S(1)}, bf16[64,40,128]{2,1,0:T(8,128)(2,1)S(1)}, u32[]{:S(2)}, u32[]{:S(2)}) collective-permute-start(bf16[64,40,128]{2,1,0:T(8,128)(2,1)S(1)} %all_to_all.25), channel_id=1, source_target_pairs={{0,1},{1,0},{2,3},{3,2},{4,5},{5,4},{6,7},{7,6},{8,9},{9,8},{10,11... | collective-permute-start | bytes 1966088 | tf_op jit(solution)/shard_map/ppermute | solution.py:370
  52.6 2.7 %collective-permute-start.1 = (bf16[8,512,128]{2,1,0:T(8,128)(2,1)S(1)}, bf16[8,512,128]{2,1,0:T(8,128)(2,1)S(1)}, u32[]{:S(2)}, u32[]{:S(2)}) collective-permute-start(bf16[8,512,128]{2,1,0:T(8,128)(2,1)S(1)} %all_to_all.26.q_own_ref), channel_id=1, source_target_pairs={{0,1},{1,0},{2,3},{3,2},{4,5},{5,4},{6,7},{7,6},{8,9},{9,8},{10,11... | collective-permute-start | bytes 3145736 | tf_op jit(solution)/shard_map/ppermute | solution.py:370
  55.3 1.0 copy-start.3
  71.7 23.1 %copy-start.2 = (f32[128]{0:T(128)S(1)}, f32[128]{0:T(128)}, u32[]{:S(2)}) copy-start(f32[128]{0:T(128)} %param.17) | copy-start | bytes 1540
  71.7 17.0 %collective-permute-start.2 = (bf16[8,512,128]{2,1,0:T(8,128)(2,1)S(1)}, bf16[8,512,128]{2,1,0:T(8,128)(2,1)S(1)}, u32[]{:S(2)}, u32[]{:S(2)}) collective-permute-start(bf16[8,512,128]{2,1,0:T(8,128)(2,1)S(1)} %get-tuple-element.24), channel_id=1, source_target_pairs={{0,1},{1,0},{2,3},{3,2},{4,5},{5,4},{6,7},{7,6},{8,9},{9,8},{10,11... | collective-permute-start | bytes 3145736 | tf_op jit(solution)/shard_map/ppermute | solution.py:370
  86.7 1.9 %collective-permute-start.4 = (bf16[8,256,128]{2,1,0:T(8,128)(2,1)S(1)}, bf16[8,256,128]{2,1,0:T(8,128)(2,1)S(1)}, u32[]{:S(2)}, u32[]{:S(2)}) collective-permute-start(bf16[8,256,128]{2,1,0:T(8,128)(2,1)S(1)} %all_to_all.27.kv_own_ref), channel_id=1, source_target_pairs={{0,1},{1,0},{2,3},{3,2},{4,5},{5,4},{6,7},{7,6},{8,9},{9,8},{10,11... | collective-permute-start | bytes 1572872 | tf_op jit(solution)/shard_map/ppermute | solution.py:370
  86.7 2.0 %collective-permute-start.3 = (f32[8,8,128]{2,1,0:T(8,128)S(1)}, f32[8,8,128]{2,1,0:T(8,128)S(1)}, u32[]{:S(2)}, u32[]{:S(2)}) collective-permute-start(f32[8,8,128]{2,1,0:T(8,128)S(1)} %get-tuple-element.25.lse_ref), channel_id=1, source_target_pairs={{0,1},{1,0},{2,3},{3,2},{4,5},{5,4},{6,7},{7,6},{8,9},{9,8},{10,11... | collective-permute-start | bytes 98312 | tf_op jit(solution)/shard_map/ppermute | solution.py:370
  91.2 21.6 %all-to-all-start.3 = ((bf16[8,528,128]{2,1,0:T(8,128)(2,1)}), bf16[8,528,128]{2,1,0:T(8,128)(2,1)S(1)}, u32[]{:S(2)}, u32[]{:S(2)}) async-start(bf16[8,528,128]{2,1,0:T(8,128)(2,1)} %get-tuple-element.27), calls=%async_computation.3 | async-start | bytes 2162688 | tf_op jit(solution)/shard_map/all_to_all | solution.py:374
  112.8 23.0 %copy-start = (s32[8]{0:T(128)S(1)}, s32[8]{0:T(128)}, u32[]{:S(2)}) copy-start(s32[8]{0:T(128)} %owner_ref.3) | copy-start | bytes 100
  115.9 2.0 %collective-permute-start.5 = (bf16[8,8,16,256]{3,2,1,0:T(8,128)(2,1)S(1)}, bf16[8,8,16,256]{3,2,1,0:T(8,128)(2,1)S(1)}, u32[]{:S(2)}, u32[]{:S(2)}) collective-permute-start(bf16[8,8,16,256]{3,2,1,0:T(8,128)(2,1)S(1)} %get-tuple-element.34), channel_id=1, source_target_pairs={{0,1},{1,0},{2,3},{3,2},{4,5},{5,4},{6,7},{7,6},{8,9},{9,8},{10,11... | collective-permute-start | bytes 1572872 | tf_op jit(solution)/shard_map/ppermute | solution.py:370
where the time goes:
time: 137 us
  blocking collectives  79.2 us (58%)
  Pallas kernels  28.5 us (21%)
  waiting for transfers between devices  24.1 us (18%)
  starting transfers between devices  4.24 us (3%)
    all_to_all x4, blocking collectives, exchange(): return lax.all_to_all(x, axes, split_axis=0, concat_axis=0, tiled=True)  79.2 us
    all_to_all x1, waiting for transfers between devices, exchange(): return lax.all_to_all(x, axes, split_axis=0, concat_axis=0, tiled=True)  16 us
    pallas_call x1, Pallas kernels, local(): attend(cache_lengths, q_own, far(q_other), far(cache_keys), far(cache_val...  15.4 us
    ppermute x6, waiting for transfers between devices, swap(): return lax.ppermute(x, 'core', [(0, 1), (1, 0)])  8.1 us
    all_to_all x1, starting transfers between devices, exchange(): return lax.all_to_all(x, axes, split_axis=0, concat_axis=0, tiled=True)  3.56 us
    pallas_call x1, Pallas kernels, local(): pl.pallas_call(finish_kernel, compiler_params=pltpu.CompilerParams(vmem_l...  3.09 us
    pallas_call x1, Pallas kernels, local(): pl.pallas_call(query_kernel, compiler_params=pltpu.CompilerParams(vmem_li...  2.99 us
  transfers between devices with their start and end apart: 7, of which 5 were waited for; matrix products, arithmetic and copies ran while one was open for 0% of the time, Pallas kernels for 2%

commit v1 on v0

--- a/solution.py
+++ b/solution.py
@@ -1,4 +1,3 @@
-import functools
 import math
 
 import jax
@@ -70,25 +69,21 @@
     other_ref,
     gain_far,
     wq_far,
-    wkv_far,
     qgain_far,
-    out_ref,
-    kv_ref,
     mine_ref,
+    slice_ref,
     marks_ref,
     gain_ref,
     wq_ref,
-    wkv_ref,
     qgain_ref,
     sem,
 ):
     gain_copy = pltpu.make_async_copy(gain_far, gain_ref, sem.at[0])
     qgain_copy = pltpu.make_async_copy(qgain_far, qgain_ref, sem.at[1])
-    wkv_copy = pltpu.make_async_copy(wkv_far, wkv_ref, sem.at[2])
     wq_copies = [
-        pltpu.make_async_copy(wq_far.at[c], wq_ref.at[c], sem.at[3 + c]) for c in range(CHIPS)
+        pltpu.make_async_copy(wq_far.at[c], wq_ref.at[c], sem.at[2 + c]) for c in range(CHIPS)
     ]
-    for copy in [gain_copy, qgain_copy] + wq_copies + [wkv_copy]:
+    for copy in [gain_copy, qgain_copy] + wq_copies:
         copy.start()
     core = lax.axis_index("core")
     chip = lax.axis_index("chip")
@@ -122,43 +117,49 @@
         for b in range(WIDE):
             start = b * ROWS + j * DRAFT
             mine_ref[start : start + DRAFT, :] = head[b]
-            for c in range(CHIPS):
-                out_ref[c, start : start + DRAFT, :] = head[b]
     for b in range(WIDE):
         marks_ref[b] = own_ref[b, 0, 32:40, :]
-    wkv_copy.wait()
-    keyval = jnp.dot(normed(own_ref, chip, core), wkv_ref[...], preferred_element_type=F32)
+    slice_ref[...] = normed(own_ref, chip, core)
+
+
+def keyval_kernel(slice_ref, wkv_ref, kv_ref):
+    tokens = WIDE * DRAFT
+    keyval = jnp.dot(slice_ref[...], wkv_ref[...], preferred_element_type=F32).astype(BF16)
     for c in range(CHIPS):
         kv = c // (CHIPS // KVH)
-        keys = keyval[:, kv * HD : (kv + 1) * HD]
-        values = keyval[:, (KVH + kv) * HD : (KVH + kv + 1) * HD]
-        kv_ref[c, 0:tokens, :] = keys.astype(BF16)
-        kv_ref[c, tokens : 2 * tokens, :] = values.astype(BF16)
-
-
-def attend_kernel(
-    first, length_ref, q_own_ref, q_other_ref, key_ref, value_ref, o_own_ref, o_other_ref, lse_ref,
-    s_ref, p_ref, m_ref,
-):
+        kv_ref[c, 0:tokens, :] = keyval[:, kv * HD : (kv + 1) * HD]
+        kv_ref[c, tokens : 2 * tokens, :] = keyval[:, (KVH + kv) * HD : (KVH + kv + 1) * HD]
+
+
+def attend_kernel(length_ref, *refs):
+    q_refs, refs = refs[: CHIPS * CORES], refs[CHIPS * CORES :]
+    key_ref, value_ref, o_own_ref, o_other_ref, lse_ref, s_ref, p_ref, m_ref = refs
     b = pl.program_id(0)
+    chip = lax.axis_index("chip")
+    odd = lax.rem(chip, 2)
     span = key_ref.shape[1]
     tile = 2 * HD
     tiles = span // tile
-    index = lax.axis_index("chip") * CORES + lax.axis_index("core")
-    live = length_ref[first + b] - index * span
+    index = chip * CORES + lax.axis_index("core")
+    live = length_ref[b] - index * span
     ones = jnp.ones((span, HD), BF16)
     rows = lax.broadcasted_iota(jnp.int32, (HD, HD), 0)
     lanes = lax.broadcasted_iota(jnp.int32, (HD, HD), 1)
 
+    def head(kv):
+        return jnp.bitwise_xor(chip // 2, kv)
+
+    def columns(kv):
+        return pl.ds(pl.multiple_of(head(kv) * HD, HD), HD)
+
     def query(kv):
-        return jnp.concatenate(
-            [q_own_ref[2 * kv], q_own_ref[2 * kv + 1], q_other_ref[2 * kv], q_other_ref[2 * kv + 1]],
-            axis=0,
-        )
+        picked = [2 * kv, 2 * kv + 1, CHIPS + 2 * kv, CHIPS + 2 * kv + 1]
+        here = pl.ds(pl.multiple_of(b * ROWS, ROWS), ROWS)
+        return jnp.concatenate([q_refs[i][here, :] for i in picked], axis=0)
 
     def score(kv, i, q, top, masked):
         at = slice(i * tile, (i + 1) * tile)
-        keys = key_ref[0, at, kv * HD : (kv + 1) * HD]
+        keys = key_ref[0, at, columns(kv)]
         part = lax.dot_general(q, keys, (((1,), (1,)), ((), ())), preferred_element_type=F32)
         if masked:
             place = lax.broadcasted_iota(jnp.int32, (1, tile), 1) + i * tile
@@ -168,42 +169,43 @@
         return high if top is None else jnp.maximum(top, high)
 
     def close(kv, top):
-        m_ref[kv % 2] = jnp.broadcast_to(jnp.max(top, axis=-1, keepdims=True), top.shape)
+        m_ref[kv] = jnp.broadcast_to(jnp.max(top, axis=-1, keepdims=True), top.shape)
 
     def soft(kv, i):
         count = KVH * ROWS // tiles
         at = slice(i * count, (i + 1) * count)
-        top = m_ref[kv % 2, at, :]
+        top = m_ref[kv, at, :]
         for j in range(span // HD):
             part = s_ref[kv % 2, at, j * HD : (j + 1) * HD]
             p_ref[kv % 2, at, j * HD : (j + 1) * HD] = jnp.exp2((part - top) * SCALE2).astype(BF16)
 
     def value(kv):
-        values = jnp.concatenate([value_ref[0, :, kv * HD : (kv + 1) * HD], ones], axis=1)
+        values = jnp.concatenate([value_ref[0, :, columns(kv)], ones], axis=1)
         summed = jnp.dot(p_ref[kv % 2], values, preferred_element_type=F32)
         den = summed[:, HD:]
         out = (summed[:, :HD] / den).astype(BF16)
-        o_own_ref[2 * kv] = out[0 * ROWS : 1 * ROWS]
-        o_own_ref[2 * kv + 1] = out[1 * ROWS : 2 * ROWS]
-        o_other_ref[2 * kv] = out[2 * ROWS : 3 * ROWS]
-        o_other_ref[2 * kv + 1] = out[3 * ROWS : 4 * ROWS]
-        lse = m_ref[kv % 2] * SCALE2 + jnp.log2(den)
+        for i in range(2):
+            target = jnp.bitwise_xor(chip, 2 * kv + i)
+            o_own_ref[target] = out[i * ROWS : (i + 1) * ROWS]
+            o_other_ref[target] = out[(2 + i) * ROWS : (3 + i) * ROWS]
+        lse = m_ref[kv] * SCALE2 + jnp.log2(den)
         for side in range(2):
             block = lse[side * HD : (side + 1) * HD]
             line = jnp.sum(jnp.where(rows == lanes, block, 0.0), axis=0, keepdims=True)
-            lse_ref[0, side * KVH + kv : side * KVH + kv + 1, :] = line
+            line = jnp.where(odd == 1, pltpu.roll(line, ROWS, 1), line)
+            lse_ref[0, pl.ds(side * KVH + head(kv), 1), :] = line
 
     def whole(masked):
-        for stage in range(KVH + 1):
+        for stage in range(KVH + 2):
             top = None
             q = query(stage) if stage < KVH else None
+            if stage > 1:
+                value(stage - 2)
             for i in range(tiles):
                 if stage < KVH:
                     top = score(stage, i, q, top, masked)
-                if stage > 0:
+                if 0 < stage <= KVH:
                     soft(stage - 1, i)
-            if stage > 0:
-                value(stage - 1)
             if stage < KVH:
                 close(stage, top)
 
@@ -222,9 +224,7 @@
         whole(True)
 
 
-def join_kernel(
-    mine_ref, theirs_ref, lse_ref, lse_in_ref, kv_own_ref, kv_other_ref, out_ref, kv_ref
-):
+def join_kernel(mine_ref, theirs_ref, lse_ref, lse_in_ref, out_ref):
     one = lse_ref[:, 0:KVH, :].reshape(WIDE * KVH, HD)
     two = lse_in_ref[:, KVH : 2 * KVH, :].reshape(WIDE * KVH, HD)
     top = jnp.maximum(one, two)
@@ -267,17 +267,16 @@
                 [jnp.where(lanes < ROWS, a, m), jnp.where(lanes < ROWS, z, 0.0)], axis=0
             )
             out_ref[2 * kv + p, base : base + 2 * WIDE, :] = tail.astype(BF16)
-    total = jnp.zeros(kv_ref.shape, F32)
+
+
+def draft_kernel(q_ref, kv_own_ref, kv_other_ref, kgain_ref, mask_ref, out_ref, lse_ref):
+    tokens = WIDE * DRAFT
+    total = jnp.zeros((2 * tokens, HD), F32)
     for ref in (kv_own_ref, kv_other_ref):
         for c in range(CHIPS):
             total = total + ref[c].astype(F32)
-    kv_ref[...] = total
-
-
-def draft_kernel(q_ref, kv_ref, kgain_ref, mask_ref, out_ref, lse_ref):
-    tokens = WIDE * DRAFT
-    keys = rms(kv_ref[0:tokens, :], kgain_ref[...]).astype(BF16)
-    values = kv_ref[tokens : 2 * tokens, :].astype(BF16)
+    keys = rms(total[:tokens], kgain_ref[...]).astype(BF16)
+    values = total[tokens:].astype(BF16)
     lanes = lax.broadcasted_iota(jnp.int32, (DRAFT, HD), 1)
     for b in range(WIDE):
         at = slice(b * ROWS, (b + 1) * ROWS)
@@ -370,6 +369,10 @@
     return lax.ppermute(x, "core", [(0, 1), (1, 0)])
 
 
+def hop(x, distance):
+    return lax.ppermute(x, "chip", [(c, c ^ distance) for c in range(CHIPS)])
+
+
 def exchange(x, axes):
     return lax.all_to_all(x, axes, split_axis=0, concat_axis=0, tiled=True)
 
@@ -406,41 +409,51 @@
     arrived = arrived.reshape(WIDE, CHIPS, 40, HD)
     partner = partner.reshape(WIDE, CHIPS, 40, HD)
 
-    queries, keyval, mine, marks = pl.pallas_call(
+    mine, piece_normed, marks = pl.pallas_call(
         query_kernel,
         compiler_params=pltpu.CompilerParams(vmem_limit_bytes=16 * 1024 * 1024),
         out_shape=(
-            shape((CHIPS, WIDE * ROWS, HD), BF16),
-            shape((CHIPS, 2 * tokens, HD), BF16),
             shape((WIDE * ROWS, HD), BF16),
+            shape((tokens, piece), BF16),
             shape((WIDE, DRAFT // 2, HD), BF16),
         ),
-        in_specs=[vmem()] * 2 + [anywhere()] * 4,
-        out_specs=(vmem(),) * 4,
+        in_specs=[vmem()] * 2 + [anywhere()] * 3,
+        out_specs=(vmem(),) * 3,
         scratch_shapes=[
             pltpu.VMEM((CHIPS * CORES * 2, HD), F32),
             pltpu.VMEM((CHIPS, CORES, piece, PER_HEAD * HD), BF16),
-            pltpu.VMEM((piece, 2 * KVH * HD), BF16),
             pltpu.VMEM((1, HD), F32),
-            pltpu.SemaphoreType.DMA((3 + CHIPS,)),
+            pltpu.SemaphoreType.DMA((2 + CHIPS,)),
         ],
     )(
         arrived,
         partner,
         far(norm_gain.reshape(CHIPS * CORES * 2, HD)),
         far(w_query.reshape(CHIPS, CORES, piece, PER_HEAD * HD)),
-        far(w_keyval),
         far(query_gain.reshape(1, HD)),
     )
-    q_own = exchange(queries, "chip")
-    q_own, keyval = lax.optimization_barrier((q_own, keyval))
+    keyval = pl.pallas_call(
+        keyval_kernel,
+        compiler_params=pltpu.CompilerParams(vmem_limit_bytes=4 * 1024 * 1024),
+        cost_estimate=pl.CostEstimate(flops=70000000, bytes_accessed=1200000, transcendentals=0),
+        out_shape=shape((CHIPS, 2 * tokens, HD), BF16),
+        in_specs=[vmem()] * 2,
+        out_specs=vmem(),
+    )(piece_normed, far(w_keyval))
+    across = hop(mine, 4)
+    near = [mine] + [hop(mine, d) for d in (1, 2, 3)]
+    last = hop(across, 3)
+    away = [across] + [hop(across, d) for d in (1, 2)] + [last]
+    q_own = near + away
+    q_other = [swap(x) for x in q_own[:5]]
+    q_other.append(swap(q_own[5]))
+    q_other += [swap(x) for x in q_own[6:]]
     kv_own = exchange(keyval, "chip")
-    q_other = swap(q_own)
-
-    q_spec = pl.BlockSpec((CHIPS, ROWS, HD), lambda b: (0, b, 0))
+
+    o_spec = pl.BlockSpec((CHIPS, ROWS, HD), lambda b: (0, b, 0))
     kv_spec = pl.BlockSpec((1, span, KVH * HD), lambda b: (b, 0, 0))
     attend = pl.pallas_call(
-        functools.partial(attend_kernel, 0),
+        attend_kernel,
         cost_estimate=pl.CostEstimate(
             flops=8 * WIDE * KVH * KVH * ROWS * span * HD,
             bytes_accessed=4 * WIDE * span * KVH * HD,
@@ -450,7 +463,7 @@
         scratch_shapes=[
             pltpu.VMEM((2, KVH * ROWS, span), F32),
             pltpu.VMEM((2, KVH * ROWS, span), BF16),
-            pltpu.VMEM((2, KVH * ROWS, HD), F32),
+            pltpu.VMEM((KVH, KVH * ROWS, HD), F32),
         ],
         out_shape=(
             shape((CHIPS, WIDE * ROWS, HD), BF16),
@@ -458,24 +471,21 @@
             shape((WIDE, 2 * KVH, HD), F32),
         ),
         grid=(WIDE,),
-        in_specs=[smem(), q_spec, q_spec, kv_spec, kv_spec],
-        out_specs=(q_spec, q_spec, pl.BlockSpec((1, 2 * KVH, HD), lambda b: (b, 0, 0))),
+        in_specs=[smem()] + [vmem()] * (CHIPS * CORES) + [kv_spec] * 2,
+        out_specs=(o_spec, o_spec, pl.BlockSpec((1, 2 * KVH, HD), lambda b: (b, 0, 0))),
     )
     o_own, o_other, lse = attend(
-        cache_lengths, q_own, far(q_other), far(cache_keys), far(cache_values)
+        cache_lengths, *q_own, *q_other, far(cache_keys), far(cache_values)
     )
 
     kv_other = swap(kv_own)
-    joined, keyval = pl.pallas_call(
+    joined = pl.pallas_call(
         join_kernel,
         compiler_params=pltpu.CompilerParams(vmem_limit_bytes=8 * 1024 * 1024),
-        out_shape=(
-            shape((CHIPS, WIDE * ROWS + 2 * WIDE, HD), BF16),
-            shape((2 * tokens, HD), F32),
-        ),
-        in_specs=[vmem()] * 6,
-        out_specs=(vmem(), vmem()),
-    )(o_own, swap(o_other), lse, swap(lse), kv_own, kv_other)
+        out_shape=shape((CHIPS, WIDE * ROWS + 2 * WIDE, HD), BF16),
+        in_specs=[vmem()] * 4,
+        out_specs=vmem(),
+    )(o_own, swap(o_other), lse, swap(lse))
     parts = exchange(joined, "chip")
 
     drafted, draft_lse = pl.pallas_call(
@@ -485,9 +495,9 @@
             flops=4000000000, bytes_accessed=2000000, transcendentals=70000
         ),
         out_shape=(shape((WIDE * ROWS, HD), F32),) * 2,
-        in_specs=[vmem()] * 4,
+        in_specs=[vmem()] * 5,
         out_specs=(vmem(), vmem()),
-    )(mine, keyval, key_gain.reshape(1, HD), marks)
+    )(mine, far(kv_own), far(kv_other), key_gain.reshape(1, HD), marks)
 
     out_own, out_other = pl.pallas_call(
         finish_kernel,

time: 137 us -> 134 us (0.978)
  blocking collectives: 79.2 us -> 43 us
  starting transfers between devices: 4.24 us -> 18.8 us
  waiting for transfers between devices: 24.1 us -> 38.2 us
  Pallas kernels: 28.5 us -> 32.4 us
    all_to_all x4 -> x2, blocking collectives: 79.2 us -> 43 us  [exchange(): return lax.all_to_all(x, axes, split_axis=0, concat_axis=0, tiled=True)]
    ppermute x0 -> x7, waiting for transfers between devices: none -> 10.2 us  [hop(): return lax.ppermute(x, 'chip', [(c, c ^ distance) for c in range(CHIPS)])]
    ppermute x0 -> x7, starting transfers between devices: none -> 8.98 us  [hop(): return lax.ppermute(x, 'chip', [(c, c ^ distance) for c in range(CHIPS)])]
    all_to_all x1 -> x2, starting transfers between devices: 3.56 us -> 7.7 us  [exchange(): return lax.all_to_all(x, axes, split_axis=0, concat_axis=0, tiled=True)]
    all_to_all x1 -> x2, waiting for transfers between devices: 16 us -> 19.8 us  [exchange(): return lax.all_to_all(x, axes, split_axis=0, concat_axis=0, tiled=True)]
    pallas_call x1 -> x2, Pallas kernels: 15.4 us -> 18.4 us  [the longest x1 16.3 us: local(): attend(cache_lengths, *q_own, *q_other, far(cache_keys), far(cache_values))]
    ppermute x6 -> x13, starting transfers between devices: 0.69 us -> 2.12 us  [swap(): return lax.ppermute(x, 'core', [(0, 1), (1, 0)])]
    ppermute x6 -> x13, waiting for transfers between devices: 8.1 us -> 8.23 us  [swap(): return lax.ppermute(x, 'core', [(0, 1), (1, 0)])]
  transfers between devices with their start and end apart: 7 -> 22, of which waited for: 5 -> 13; matrix products, arithmetic and copies ran while one was open for 0% -> 0% of each run, Pallas kernels for 2% -> 6%
where the time goes in v1:
time: 134 us; the launch traced here: 133 us
  blocking collectives  43 us (32%)
  waiting for transfers between devices  38.2 us (29%)
  Pallas kernels  32.4 us (24%)
  starting transfers between devices  18.8 us (14%)
    all_to_all x2, blocking collectives, exchange(): return lax.all_to_all(x, axes, split_axis=0, concat_axis=0, tiled=True)  43 us
    all_to_all x2, waiting for transfers between devices, exchange(): return lax.all_to_all(x, axes, split_axis=0, concat_axis=0, tiled=True)  19.8 us
    pallas_call x1, Pallas kernels, local(): attend(cache_lengths, *q_own, *q_other, far(cache_keys), far(cache_values))  16.3 us
    ppermute x7, waiting for transfers between devices, hop(): return lax.ppermute(x, 'chip', [(c, c ^ distance) for c in range(CHIPS)])  10.2 us
    ppermute x7, starting transfers between devices, hop(): return lax.ppermute(x, 'chip', [(c, c ^ distance) for c in range(CHIPS)])  8.98 us
    ppermute x13, waiting for transfers between devices, swap(): return lax.ppermute(x, 'core', [(0, 1), (1, 0)])  8.23 us
    all_to_all x2, starting transfers between devices, exchange(): return lax.all_to_all(x, axes, split_axis=0, concat_axis=0, tiled=True)  7.7 us
    pallas_call x1, Pallas kernels, local(): pl.pallas_call(draft_kernel, compiler_params=pltpu.CompilerParams(vmem_li...  3.33 us
  transfers between devices with their start and end apart: 22, of which 13 were waited for; matrix products, arithmetic and copies ran while one was open for 0% of the time, Pallas kernels for 6%

profile of v1, /device:TPU:0, one launch (start us, length us, event | category | flops | bytes accessed | tf_op | source)
XLA Modules:
  0.0 133.3 jit_solution(13830298341512321517)
XLA Ops:
  0.0 0.0 copy-start.1
  0.0 1.0 shard_map.118
  1.0 25.6 %all_to_all.20 = bf16[64,40,128]{2,1,0:T(8,128)(2,1)S(1)} all-to-all(bf16[64,40,128]{2,1,0:T(8,128)(2,1)S(1)} %bitcast.9), channel_id=1, replica_groups=mesh['wide'=8,'chip'=8,'core'=2] {'wide','chip'}, dimensions={0} | all-to-all | bytes 1310720 | tf_op jit(solution)/shard_map/all_to_all | solution.py:377
  26.6 0.0 collective-permute-start
  26.6 2.1 %collective-permute-done = bf16[64,40,128]{2,1,0:T(8,128)(2,1)S(1)} collective-permute-done((bf16[64,40,128]{2,1,0:T(8,128)(2,1)S(1)}, bf16[64,40,128]{2,1,0:T(8,128)(2,1)S(1)}, u32[]{:S(2)}, u32[]{:S(2)}) %collective-permute-start) | collective-permute-done | bytes 655392 | tf_op jit(solution)/shard_map/ppermute | solution.py:369
  28.7 2.7 %shard_map.119 = (bf16[512,128]{1,0:T(8,128)(2,1)S(1)}, bf16[128,256]{1,0:T(8,128)(2,1)S(1)}, bf16[8,8,128]{2,1,0:T(8,128)(2,1)S(1)}) custom-call(bf16[8,8,40,128]{3,2,1,0:T(8,128)(2,1)S(1)} %bitcast.10, bf16[8,8,40,128]{3,2,1,0:T(8,128)(2,1)S(1)} %bitcast.13, f32[32,128]{1,0:T(8,128)} %bitcast.16, bf16[8,2,256,512]{3,2,1,0:T(8,128)(2,1)} %bitcast.15, ...), custom_call_target="tpu_custom_call" | custom-call | tf_op jit(solution)/shard_map/pallas_call | solution.py:412
  31.4 1.8 %collective-permute-start.4 = (bf16[512,128]{1,0:T(8,128)(2,1)S(1)}, bf16[512,128]{1,0:T(8,128)(2,1)S(1)}, u32[]{:S(2)}, u32[]{:S(2)}) collective-permute-start(bf16[512,128]{1,0:T(8,128)(2,1)S(1)} %get-tuple-element.15.refs_0_.q_ref), channel_id=1, source_target_pairs={{0,8},{2,10},{4,12},{6,14},{8,0},{10,2},{12,4},{14,6},{1,9},{3,11}... | collective-permute-start | bytes 393224 | tf_op jit(solution)/shard_map/ppermute | solution.py:373
  33.2 0.0 collective-permute-start.8
  33.2 1.2 collective-permute-start.3
  34.3 1.5 %collective-permute-start.2 = (bf16[512,128]{1,0:T(8,128)(2,1)S(1)}, bf16[512,128]{1,0:T(8,128)(2,1)S(1)}, u32[]{:S(2)}, u32[]{:S(2)}) collective-permute-start(bf16[512,128]{1,0:T(8,128)(2,1)S(1)} %get-tuple-element.15.refs_0_.q_ref), channel_id=1, source_target_pairs={{0,4},{2,6},{4,0},{6,2},{8,12},{10,14},{12,8},{14,10},{1,5},{3,7},... | collective-permute-start | bytes 393224 | tf_op jit(solution)/shard_map/ppermute | solution.py:373
  35.8 1.5 %collective-permute-start.1 = (bf16[512,128]{1,0:T(8,128)(2,1)S(1)}, bf16[512,128]{1,0:T(8,128)(2,1)S(1)}, u32[]{:S(2)}, u32[]{:S(2)}) collective-permute-start(bf16[512,128]{1,0:T(8,128)(2,1)S(1)} %get-tuple-element.15.refs_0_.q_ref), channel_id=1, source_target_pairs={{0,2},{2,0},{4,6},{6,4},{8,10},{10,8},{12,14},{14,12},{1,3},{3,1},... | collective-permute-start | bytes 393224 | tf_op jit(solution)/shard_map/ppermute | solution.py:373
  37.3 1.2 collective-permute-done.4.refs_4_
  38.5 0.0 collective-permute-start.12
  38.5 0.0 collective-permute-done.8.refs_8_
  38.5 1.4 %collective-permute-start.7 = (bf16[512,128]{1,0:T(8,128)(2,1)S(1)}, bf16[512,128]{1,0:T(8,128)(2,1)S(1)}, u32[]{:S(2)}, u32[]{:S(2)}) collective-permute-start(bf16[512,128]{1,0:T(8,128)(2,1)S(1)} %collective-permute-done.4.refs_4_), channel_id=1, source_target_pairs={{0,6},{2,4},{4,2},{6,0},{8,14},{10,12},{12,10},{14,8},{1,7},{3,5},... | collective-permute-start | bytes 393224 | tf_op jit(solution)/shard_map/ppermute | solution.py:373
  39.9 3.4 %collective-permute-done.3.refs_3_ = bf16[512,128]{1,0:T(8,128)(2,1)S(1)} collective-permute-done((bf16[512,128]{1,0:T(8,128)(2,1)S(1)}, bf16[512,128]{1,0:T(8,128)(2,1)S(1)}, u32[]{:S(2)}, u32[]{:S(2)}) %collective-permute-start.3) | collective-permute-done | bytes 131104 | tf_op jit(solution)/shard_map/ppermute | solution.py:373
  43.4 0.0 collective-permute-start.6
  43.4 0.0 collective-permute-done.2.refs_2_
  43.4 1.7 %collective-permute-start.5 = (bf16[512,128]{1,0:T(8,128)(2,1)S(1)}, bf16[512,128]{1,0:T(8,128)(2,1)S(1)}, u32[]{:S(2)}, u32[]{:S(2)}) collective-permute-start(bf16[512,128]{1,0:T(8,128)(2,1)S(1)} %collective-permute-done.4.refs_4_), channel_id=1, source_target_pairs={{0,2},{2,0},{4,6},{6,4},{8,10},{10,8},{12,14},{14,12},{1,3},{3,1},... | collective-permute-start | bytes 393224 | tf_op jit(solution)/shard_map/ppermute | solution.py:373
  45.1 0.0 collective-permute-done.1.refs_1_
  45.1 0.0 collective-permute-start.11
  45.1 0.0 collective-permute-done.12.refs_12_
  45.1 0.5 collective-permute-start.10
  45.6 0.3 collective-permute-done.7.refs_7_
  45.9 0.0 collective-permute-start.9
  45.9 5.1 %collective-permute-done.6.refs_6_ = bf16[512,128]{1,0:T(8,128)(2,1)S(1)} collective-permute-done((bf16[512,128]{1,0:T(8,128)(2,1)S(1)}, bf16[512,128]{1,0:T(8,128)(2,1)S(1)}, u32[]{:S(2)}, u32[]{:S(2)}) %collective-permute-start.6) | collective-permute-done | bytes 131104 | tf_op jit(solution)/shard_map/ppermute | solution.py:373
  51.1 0.0 collective-permute-start.15
  51.1 0.0 collective-permute-done.5.refs_5_
  51.1 0.5 collective-permute-start.14
  51.6 0.0 collective-permute-done.11.refs_11_
  51.6 0.1 collective-permute-start.13
  51.7 0.0 collective-permute-done.10.refs_10_
  51.7 0.0 collective-permute-done.9.refs_9_
  51.7 0.7 collective-permute-done.15.refs_15_
  52.4 0.2 collective-permute-done.14.refs_14_
  52.6 0.3 collective-permute-done.13.refs_13_
  52.9 0.0 copy-done.1
  52.9 16.3 %shard_map.120 = (bf16[8,512,128]{2,1,0:T(8,128)(2,1)S(1)}, bf16[8,512,128]{2,1,0:T(8,128)(2,1)S(1)}, f32[8,8,128]{2,1,0:T(8,128)S(1)}) custom-call(s32[8]{0:T(128)S(1)} %copy-done.1, bf16[512,128]{1,0:T(8,128)(2,1)S(1)} %get-tuple-element.15.refs_0_.q_ref, bf16[512,128]{1,0:T(8,128)(2,1)S(1)} %collective-permute-done.1.refs_1_, ...), custom_call_target="tpu_custom_call" | custom-call | flops 8589934592 | bytes 16777216 | tf_op jit(solution)/shard_map/pallas_call | solution.py:477
  69.3 0.0 copy-start.2
  69.3 0.1 collective-permute-start.16
  69.4 2.1 %shard_map.122 = bf16[8,256,128]{2,1,0:T(8,128)(2,1)} custom-call(bf16[128,256]{1,0:T(8,128)(2,1)S(1)} %get-tuple-element.19.slice_ref, bf16[256,1024]{1,0:T(8,128)(2,1)} %wkv_ref.1), custom_call_target="tpu_custom_call" | custom-call | flops 70000000 | bytes 1200000 | tf_op jit(solution)/shard_map/pallas_call | solution.py:435
  71.4 4.1 %all-to-all-start.2 = ((bf16[8,256,128]{2,1,0:T(8,128)(2,1)}), bf16[8,256,128]{2,1,0:T(8,128)(2,1)}, u32[]{:S(2)}, u32[]{:S(2)}) async-start(bf16[8,256,128]{2,1,0:T(8,128)(2,1)} %shard_map.122), calls=%async_computation.2 | async-start | bytes 1048576 | tf_op jit(solution)/shard_map/all_to_all | solution.py:377
  75.6 0.8 collective-permute-start.17
  76.3 0.9 collective-permute-done.17.lse_in_ref
  77.2 0.0 collective-permute-done.16.theirs_ref
  77.2 2.5 %shard_map.121 = bf16[8,528,128]{2,1,0:T(8,128)(2,1)} custom-call(bf16[8,512,128]{2,1,0:T(8,128)(2,1)S(1)} %get-tuple-element.16.mine_ref, bf16[8,512,128]{2,1,0:T(8,128)(2,1)S(1)} %collective-permute-done.16.theirs_ref, f32[8,8,128]{2,1,0:T(8,128)S(1)} %get-tuple-element.18.lse_ref, f32[8,8,128]{2,1,0:T(8,128)S(1)} %collective-permute-done.17.lse_in_ref), custom_call_target="tpu_custom_call" | custom-call | tf_op jit(solution)/shard_map/pallas_call | solution.py:482
  79.7 8.4 %all-to-all-done.2.kv_own_ref = bf16[8,256,128]{2,1,0:T(8,128)(2,1)} async-done(((bf16[8,256,128]{2,1,0:T(8,128)(2,1)}), bf16[8,256,128]{2,1,0:T(8,128)(2,1)}, u32[]{:S(2)}, u32[]{:S(2)}) %all-to-all-start.2) | async-done | bytes 524320 | tf_op jit(solution)/shard_map/all_to_all | solution.py:377
  88.1 3.6 %all-to-all-start.1 = ((bf16[8,528,128]{2,1,0:T(8,128)(2,1)}), bf16[8,528,128]{2,1,0:T(8,128)(2,1)S(1)}, u32[]{:S(2)}, u32[]{:S(2)}) async-start(bf16[8,528,128]{2,1,0:T(8,128)(2,1)} %shard_map.121), calls=%async_computation.1 | async-start | bytes 2162688 | tf_op jit(solution)/shard_map/all_to_all | solution.py:377
  91.7 0.1 collective-permute-start.18
  91.8 2.1 %collective-permute-done.18.kv_other_ref = bf16[8,256,128]{2,1,0:T(8,128)(2,1)S(1)} collective-permute-done((bf16[8,256,128]{2,1,0:T(8,128)(2,1)}, bf16[8,256,128]{2,1,0:T(8,128)(2,1)S(1)}, u32[]{:S(2)}, u32[]{:S(2)}) %collective-permute-start.18) | collective-permute-done | bytes 524320 | tf_op jit(solution)/shard_map/ppermute | solution.py:369
  93.9 0.0 copy-start.3
  93.9 0.8 copy-done.3
  94.7 0.0 copy-done.2
  94.7 3.3 %shard_map.123 = (f32[512,128]{1,0:T(8,128)S(1)}, f32[512,128]{1,0:T(8,128)S(1)}) custom-call(bf16[512,128]{1,0:T(8,128)(2,1)S(1)} %get-tuple-element.15.refs_0_.q_ref, bf16[8,256,128]{2,1,0:T(8,128)(2,1)} %all-to-all-done.2.kv_own_ref, bf16[8,256,128]{2,1,0:T(8,128)(2,1)} %copy-done.3, f32[1,128]{1,0:T(1,128)S(1)} %bitcast.14, ...), custom_call_target="tpu_custom_call" | custom-call | flops 4000000000 | bytes 2000000 | tf_op jit(solution)/shard_map/pallas_call | solution.py:491
  98.0 11.3 %all-to-all-done.1.part_ref = bf16[8,528,128]{2,1,0:T(8,128)(2,1)S(1)} async-done(((bf16[8,528,128]{2,1,0:T(8,128)(2,1)}), bf16[8,528,128]{2,1,0:T(8,128)(2,1)S(1)}, u32[]{:S(2)}, u32[]{:S(2)}) %all-to-all-start.1) | async-done | bytes 1081376 | tf_op jit(solution)/shard_map/all_to_all | solution.py:377
  109.4 0.0 copy-start
  109.4 3.1 %shard_map.124 = (bf16[8,8,16,256]{3,2,1,0:T(8,128)(2,1)S(1)}, bf16[8,8,16,256]{3,2,1,0:T(8,128)(2,1)S(1)}) custom-call(bf16[8,528,128]{2,1,0:T(8,128)(2,1)S(1)} %all-to-all-done.1.part_ref, f32[512,128]{1,0:T(8,128)S(1)} %get-tuple-element.21.draft_ref, f32[512,128]{1,0:T(8,128)S(1)} %get-tuple-element.22.lse_ref, bf16[512,4096]{1,0:T(8,128)(2,1)} %wo_far.1), custom_call_target="tpu_custom_call" | custom-call | tf_op jit(solution)/shard_map/pallas_call | solution.py:502
  112.4 0.1 collective-permute-start.19
  112.5 1.9 %collective-permute-done.19.two_ref = bf16[8,8,16,256]{3,2,1,0:T(8,128)(2,1)S(1)} collective-permute-done((bf16[8,8,16,256]{3,2,1,0:T(8,128)(2,1)S(1)}, bf16[8,8,16,256]{3,2,1,0:T(8,128)(2,1)S(1)}, u32[]{:S(2)}, u32[]{:S(2)}) %collective-permute-start.19) | collective-permute-done | bytes 524320 | tf_op jit(solution)/shard_map/ppermute | solution.py:369
  114.4 0.1 shard_map.125
  114.6 17.4 %all_to_all.21 = bf16[64,16,256]{2,1,0:T(8,128)(2,1)S(1)} all-to-all(bf16[64,16,256]{2,1,0:T(8,128)(2,1)S(1)} %bitcast.11), channel_id=1, replica_groups=mesh['wide'=8,'chip'=8,'core'=2] {'wide','chip'}, dimensions={0} | all-to-all | bytes 1048576 | tf_op jit(solution)/shard_map/all_to_all | solution.py:377
  132.0 0.0 copy-done
  132.0 1.2 shard_map.126
Async XLA Ops:
  0.0 52.9 %copy-start.1 = (s32[8]{0:T(128)S(1)}, s32[8]{0:T(128)}, u32[]{:S(2)}) copy-start(s32[8]{0:T(128)} %length_ref.1) | copy-start | bytes 100
  26.6 2.1 %collective-permute-start = (bf16[64,40,128]{2,1,0:T(8,128)(2,1)S(1)}, bf16[64,40,128]{2,1,0:T(8,128)(2,1)S(1)}, u32[]{:S(2)}, u32[]{:S(2)}) collective-permute-start(bf16[64,40,128]{2,1,0:T(8,128)(2,1)S(1)} %all_to_all.20), channel_id=1, source_target_pairs={{0,1},{1,0},{2,3},{3,2},{4,5},{5,4},{6,7},{7,6},{8,9},{9,8},{10,11... | collective-permute-start | bytes 1966088 | tf_op jit(solution)/shard_map/ppermute | solution.py:369
  31.4 7.1 %collective-permute-start.4 = (bf16[512,128]{1,0:T(8,128)(2,1)S(1)}, bf16[512,128]{1,0:T(8,128)(2,1)S(1)}, u32[]{:S(2)}, u32[]{:S(2)}) collective-permute-start(bf16[512,128]{1,0:T(8,128)(2,1)S(1)} %get-tuple-element.15.refs_0_.q_ref), channel_id=1, source_target_pairs={{0,8},{2,10},{4,12},{6,14},{8,0},{10,2},{12,4},{14,6},{1,9},{3,11}... | collective-permute-start | bytes 393224 | tf_op jit(solution)/shard_map/ppermute | solution.py:373
  33.2 5.4 %collective-permute-start.8 = (bf16[512,128]{1,0:T(8,128)(2,1)S(1)}, bf16[512,128]{1,0:T(8,128)(2,1)S(1)}, u32[]{:S(2)}, u32[]{:S(2)}) collective-permute-start(bf16[512,128]{1,0:T(8,128)(2,1)S(1)} %get-tuple-element.15.refs_0_.q_ref), channel_id=1, source_target_pairs={{0,1},{1,0},{2,3},{3,2},{4,5},{5,4},{6,7},{7,6},{8,9},{9,8},{10,11... | collective-permute-start | bytes 393224 | tf_op jit(solution)/shard_map/ppermute | solution.py:369
  33.2 10.2 %collective-permute-start.3 = (bf16[512,128]{1,0:T(8,128)(2,1)S(1)}, bf16[512,128]{1,0:T(8,128)(2,1)S(1)}, u32[]{:S(2)}, u32[]{:S(2)}) collective-permute-start(bf16[512,128]{1,0:T(8,128)(2,1)S(1)} %get-tuple-element.15.refs_0_.q_ref), channel_id=1, source_target_pairs={{0,6},{2,4},{4,2},{6,0},{8,14},{10,12},{12,10},{14,8},{1,7},{3,5},... | collective-permute-start | bytes 393224 | tf_op jit(solution)/shard_map/ppermute | solution.py:373
  34.3 9.0 %collective-permute-start.2 = (bf16[512,128]{1,0:T(8,128)(2,1)S(1)}, bf16[512,128]{1,0:T(8,128)(2,1)S(1)}, u32[]{:S(2)}, u32[]{:S(2)}) collective-permute-start(bf16[512,128]{1,0:T(8,128)(2,1)S(1)} %get-tuple-element.15.refs_0_.q_ref), channel_id=1, source_target_pairs={{0,4},{2,6},{4,0},{6,2},{8,12},{10,14},{12,8},{14,10},{1,5},{3,7},... | collective-permute-start | bytes 393224 | tf_op jit(solution)/shard_map/ppermute | solution.py:373
  35.8 9.3 %collective-permute-start.1 = (bf16[512,128]{1,0:T(8,128)(2,1)S(1)}, bf16[512,128]{1,0:T(8,128)(2,1)S(1)}, u32[]{:S(2)}, u32[]{:S(2)}) collective-permute-start(bf16[512,128]{1,0:T(8,128)(2,1)S(1)} %get-tuple-element.15.refs_0_.q_ref), channel_id=1, source_target_pairs={{0,2},{2,0},{4,6},{6,4},{8,10},{10,8},{12,14},{14,12},{1,3},{3,1},... | collective-permute-start | bytes 393224 | tf_op jit(solution)/shard_map/ppermute | solution.py:373
  38.5 6.6 %collective-permute-start.12 = (bf16[512,128]{1,0:T(8,128)(2,1)S(1)}, bf16[512,128]{1,0:T(8,128)(2,1)S(1)}, u32[]{:S(2)}, u32[]{:S(2)}) collective-permute-start(bf16[512,128]{1,0:T(8,128)(2,1)S(1)} %collective-permute-done.4.refs_4_), channel_id=1, source_target_pairs={{0,1},{1,0},{2,3},{3,2},{4,5},{5,4},{6,7},{7,6},{8,9},{9,8},{10,11... | collective-permute-start | bytes 393224 | tf_op jit(solution)/shard_map/ppermute | solution.py:369
  38.5 7.4 %collective-permute-start.7 = (bf16[512,128]{1,0:T(8,128)(2,1)S(1)}, bf16[512,128]{1,0:T(8,128)(2,1)S(1)}, u32[]{:S(2)}, u32[]{:S(2)}) collective-permute-start(bf16[512,128]{1,0:T(8,128)(2,1)S(1)} %collective-permute-done.4.refs_4_), channel_id=1, source_target_pairs={{0,6},{2,4},{4,2},{6,0},{8,14},{10,12},{12,10},{14,8},{1,7},{3,5},... | collective-permute-start | bytes 393224 | tf_op jit(solution)/shard_map/ppermute | solution.py:373
  43.4 7.7 %collective-permute-start.6 = (bf16[512,128]{1,0:T(8,128)(2,1)S(1)}, bf16[512,128]{1,0:T(8,128)(2,1)S(1)}, u32[]{:S(2)}, u32[]{:S(2)}) collective-permute-start(bf16[512,128]{1,0:T(8,128)(2,1)S(1)} %collective-permute-done.4.refs_4_), channel_id=1, source_target_pairs={{0,4},{2,6},{4,0},{6,2},{8,12},{10,14},{12,8},{14,10},{1,5},{3,7},... | collective-permute-start | bytes 393224 | tf_op jit(solution)/shard_map/ppermute | solution.py:373
  43.4 7.7 %collective-permute-start.5 = (bf16[512,128]{1,0:T(8,128)(2,1)S(1)}, bf16[512,128]{1,0:T(8,128)(2,1)S(1)}, u32[]{:S(2)}, u32[]{:S(2)}) collective-permute-start(bf16[512,128]{1,0:T(8,128)(2,1)S(1)} %collective-permute-done.4.refs_4_), channel_id=1, source_target_pairs={{0,2},{2,0},{4,6},{6,4},{8,10},{10,8},{12,14},{14,12},{1,3},{3,1},... | collective-permute-start | bytes 393224 | tf_op jit(solution)/shard_map/ppermute | solution.py:373
  45.1 6.5 %collective-permute-start.11 = (bf16[512,128]{1,0:T(8,128)(2,1)S(1)}, bf16[512,128]{1,0:T(8,128)(2,1)S(1)}, u32[]{:S(2)}, u32[]{:S(2)}) collective-permute-start(bf16[512,128]{1,0:T(8,128)(2,1)S(1)} %collective-permute-done.3.refs_3_), channel_id=1, source_target_pairs={{0,1},{1,0},{2,3},{3,2},{4,5},{5,4},{6,7},{7,6},{8,9},{9,8},{10,11... | collective-permute-start | bytes 393224 | tf_op jit(solution)/shard_map/ppermute | solution.py:369
  45.1 6.6 %collective-permute-start.10 = (bf16[512,128]{1,0:T(8,128)(2,1)S(1)}, bf16[512,128]{1,0:T(8,128)(2,1)S(1)}, u32[]{:S(2)}, u32[]{:S(2)}) collective-permute-start(bf16[512,128]{1,0:T(8,128)(2,1)S(1)} %collective-permute-done.2.refs_2_), channel_id=1, source_target_pairs={{0,1},{1,0},{2,3},{3,2},{4,5},{5,4},{6,7},{7,6},{8,9},{9,8},{10,11... | collective-permute-start | bytes 393224 | tf_op jit(solution)/shard_map/ppermute | solution.py:369
  45.9 5.8 %collective-permute-start.9 = (bf16[512,128]{1,0:T(8,128)(2,1)S(1)}, bf16[512,128]{1,0:T(8,128)(2,1)S(1)}, u32[]{:S(2)}, u32[]{:S(2)}) collective-permute-start(bf16[512,128]{1,0:T(8,128)(2,1)S(1)} %collective-permute-done.1.refs_1_), channel_id=1, source_target_pairs={{0,1},{1,0},{2,3},{3,2},{4,5},{5,4},{6,7},{7,6},{8,9},{9,8},{10,11... | collective-permute-start | bytes 393224 | tf_op jit(solution)/shard_map/ppermute | solution.py:369
  51.1 1.3 %collective-permute-start.15 = (bf16[512,128]{1,0:T(8,128)(2,1)S(1)}, bf16[512,128]{1,0:T(8,128)(2,1)S(1)}, u32[]{:S(2)}, u32[]{:S(2)}) collective-permute-start(bf16[512,128]{1,0:T(8,128)(2,1)S(1)} %collective-permute-done.7.refs_7_), channel_id=1, source_target_pairs={{0,1},{1,0},{2,3},{3,2},{4,5},{5,4},{6,7},{7,6},{8,9},{9,8},{10,11... | collective-permute-start | bytes 393224 | tf_op jit(solution)/shard_map/ppermute | solution.py:369
  51.1 1.5 %collective-permute-start.14 = (bf16[512,128]{1,0:T(8,128)(2,1)S(1)}, bf16[512,128]{1,0:T(8,128)(2,1)S(1)}, u32[]{:S(2)}, u32[]{:S(2)}) collective-permute-start(bf16[512,128]{1,0:T(8,128)(2,1)S(1)} %collective-permute-done.6.refs_6_), channel_id=1, source_target_pairs={{0,1},{1,0},{2,3},{3,2},{4,5},{5,4},{6,7},{7,6},{8,9},{9,8},{10,11... | collective-permute-start | bytes 393224 | tf_op jit(solution)/shard_map/ppermute | solution.py:369
  51.6 1.3 %collective-permute-start.13 = (bf16[512,128]{1,0:T(8,128)(2,1)S(1)}, bf16[512,128]{1,0:T(8,128)(2,1)S(1)}, u32[]{:S(2)}, u32[]{:S(2)}) collective-permute-start(bf16[512,128]{1,0:T(8,128)(2,1)S(1)} %collective-permute-done.5.refs_5_), channel_id=1, source_target_pairs={{0,1},{1,0},{2,3},{3,2},{4,5},{5,4},{6,7},{7,6},{8,9},{9,8},{10,11... | collective-permute-start | bytes 393224 | tf_op jit(solution)/shard_map/ppermute | solution.py:369
  69.3 25.4 %copy-start.2 = (f32[128]{0:T(128)S(1)}, f32[128]{0:T(128)}, u32[]{:S(2)}) copy-start(f32[128]{0:T(128)} %param.17) | copy-start | bytes 1540
  69.3 7.9 %collective-permute-start.16 = (bf16[8,512,128]{2,1,0:T(8,128)(2,1)S(1)}, bf16[8,512,128]{2,1,0:T(8,128)(2,1)S(1)}, u32[]{:S(2)}, u32[]{:S(2)}) collective-permute-start(bf16[8,512,128]{2,1,0:T(8,128)(2,1)S(1)} %get-tuple-element.17), channel_id=1, source_target_pairs={{0,1},{1,0},{2,3},{3,2},{4,5},{5,4},{6,7},{7,6},{8,9},{9,8},{10,11... | collective-permute-start | bytes 3145736 | tf_op jit(solution)/shard_map/ppermute | solution.py:369
  71.4 16.7 %all-to-all-start.2 = ((bf16[8,256,128]{2,1,0:T(8,128)(2,1)}), bf16[8,256,128]{2,1,0:T(8,128)(2,1)}, u32[]{:S(2)}, u32[]{:S(2)}) async-start(bf16[8,256,128]{2,1,0:T(8,128)(2,1)} %shard_map.122), calls=%async_computation.2 | async-start | bytes 1048576 | tf_op jit(solution)/shard_map/all_to_all | solution.py:377
  75.6 1.6 %collective-permute-start.17 = (f32[8,8,128]{2,1,0:T(8,128)S(1)}, f32[8,8,128]{2,1,0:T(8,128)S(1)}, u32[]{:S(2)}, u32[]{:S(2)}) collective-permute-start(f32[8,8,128]{2,1,0:T(8,128)S(1)} %get-tuple-element.18.lse_ref), channel_id=1, source_target_pairs={{0,1},{1,0},{2,3},{3,2},{4,5},{5,4},{6,7},{7,6},{8,9},{9,8},{10,11... | collective-permute-start | bytes 98312 | tf_op jit(solution)/shard_map/ppermute | solution.py:369
  88.1 21.2 %all-to-all-start.1 = ((bf16[8,528,128]{2,1,0:T(8,128)(2,1)}), bf16[8,528,128]{2,1,0:T(8,128)(2,1)S(1)}, u32[]{:S(2)}, u32[]{:S(2)}) async-start(bf16[8,528,128]{2,1,0:T(8,128)(2,1)} %shard_map.121), calls=%async_computation.1 | async-start | bytes 2162688 | tf_op jit(solution)/shard_map/all_to_all | solution.py:377
  91.7 2.2 %collective-permute-start.18 = (bf16[8,256,128]{2,1,0:T(8,128)(2,1)}, bf16[8,256,128]{2,1,0:T(8,128)(2,1)S(1)}, u32[]{:S(2)}, u32[]{:S(2)}) collective-permute-start(bf16[8,256,128]{2,1,0:T(8,128)(2,1)} %all-to-all-done.2.kv_own_ref), channel_id=1, source_target_pairs={{0,1},{1,0},{2,3},{3,2},{4,5},{5,4},{6,7},{7,6},{8,9},{9,8},{10,11... | collective-permute-start | bytes 1572872 | tf_op jit(solution)/shard_map/ppermute | solution.py:369
  93.9 0.8 copy-start.3
  109.4 22.7 %copy-start = (s32[8]{0:T(128)S(1)}, s32[8]{0:T(128)}, u32[]{:S(2)}) copy-start(s32[8]{0:T(128)} %owner_ref.3) | copy-start | bytes 100
  112.4 2.0 %collective-permute-start.19 = (bf16[8,8,16,256]{3,2,1,0:T(8,128)(2,1)S(1)}, bf16[8,8,16,256]{3,2,1,0:T(8,128)(2,1)S(1)}, u32[]{:S(2)}, u32[]{:S(2)}) collective-permute-start(bf16[8,8,16,256]{3,2,1,0:T(8,128)(2,1)S(1)} %get-tuple-element.24), channel_id=1, source_target_pairs={{0,1},{1,0},{2,3},{3,2},{4,5},{5,4},{6,7},{7,6},{8,9},{9,8},{10,11... | collective-permute-start | bytes 1572872 | tf_op jit(solution)/shard_map/ppermute | solution.py:369

commit v2 on v1

--- a/solution.py
+++ b/solution.py
@@ -17,6 +17,7 @@
 CORES = 2
 PER_HEAD = HQ // (CHIPS * CORES)
 ROWS = PER_HEAD * DRAFT
+TOGETHER = 2
 
 EPS = 1e-06
 DEAD = -1e30
@@ -134,94 +135,111 @@
 def attend_kernel(length_ref, *refs):
     q_refs, refs = refs[: CHIPS * CORES], refs[CHIPS * CORES :]
     key_ref, value_ref, o_own_ref, o_other_ref, lse_ref, s_ref, p_ref, m_ref = refs
-    b = pl.program_id(0)
+    step = pl.program_id(0)
     chip = lax.axis_index("chip")
     odd = lax.rem(chip, 2)
     span = key_ref.shape[1]
     tile = 2 * HD
     tiles = span // tile
     index = chip * CORES + lax.axis_index("core")
-    live = length_ref[b] - index * span
     ones = jnp.ones((span, HD), BF16)
     rows = lax.broadcasted_iota(jnp.int32, (HD, HD), 0)
     lanes = lax.broadcasted_iota(jnp.int32, (HD, HD), 1)
 
+    def living(sub):
+        return length_ref[step * TOGETHER + sub] - index * span
+
     def head(kv):
         return jnp.bitwise_xor(chip // 2, kv)
 
     def columns(kv):
         return pl.ds(pl.multiple_of(head(kv) * HD, HD), HD)
 
-    def query(kv):
+    def query(sub, kv):
         picked = [2 * kv, 2 * kv + 1, CHIPS + 2 * kv, CHIPS + 2 * kv + 1]
-        here = pl.ds(pl.multiple_of(b * ROWS, ROWS), ROWS)
+        here = pl.ds(pl.multiple_of((step * TOGETHER + sub) * ROWS, ROWS), ROWS)
         return jnp.concatenate([q_refs[i][here, :] for i in picked], axis=0)
 
-    def score(kv, i, q, top, masked):
+    def score(u, sub, kv, i, q, top, live):
         at = slice(i * tile, (i + 1) * tile)
-        keys = key_ref[0, at, columns(kv)]
+        keys = key_ref[sub, at, columns(kv)]
         part = lax.dot_general(q, keys, (((1,), (1,)), ((), ())), preferred_element_type=F32)
-        if masked:
+        if live is not None:
             place = lax.broadcasted_iota(jnp.int32, (1, tile), 1) + i * tile
             part = jnp.where(place < live, part, DEAD)
-        s_ref[kv % 2, :, at] = part
+        s_ref[u % 2, :, at] = part
         high = jnp.maximum(part[:, :HD], part[:, HD:])
         return high if top is None else jnp.maximum(top, high)
 
-    def close(kv, top):
-        m_ref[kv] = jnp.broadcast_to(jnp.max(top, axis=-1, keepdims=True), top.shape)
-
-    def soft(kv, i):
+    def close(u, top):
+        m_ref[u % 4] = jnp.broadcast_to(jnp.max(top, axis=-1, keepdims=True), top.shape)
+
+    def soft(u, i):
         count = KVH * ROWS // tiles
         at = slice(i * count, (i + 1) * count)
-        top = m_ref[kv, at, :]
+        top = m_ref[u % 4, at, :]
         for j in range(span // HD):
-            part = s_ref[kv % 2, at, j * HD : (j + 1) * HD]
-            p_ref[kv % 2, at, j * HD : (j + 1) * HD] = jnp.exp2((part - top) * SCALE2).astype(BF16)
-
-    def value(kv):
-        values = jnp.concatenate([value_ref[0, :, columns(kv)], ones], axis=1)
-        summed = jnp.dot(p_ref[kv % 2], values, preferred_element_type=F32)
+            part = s_ref[u % 2, at, j * HD : (j + 1) * HD]
+            p_ref[u % 2, at, j * HD : (j + 1) * HD] = jnp.exp2((part - top) * SCALE2).astype(BF16)
+
+    def value(u, sub, kv):
+        values = jnp.concatenate([value_ref[sub, :, columns(kv)], ones], axis=1)
+        summed = jnp.dot(p_ref[u % 2], values, preferred_element_type=F32)
         den = summed[:, HD:]
         out = (summed[:, :HD] / den).astype(BF16)
+        here = pl.ds(pl.multiple_of(sub * ROWS, ROWS), ROWS)
         for i in range(2):
             target = jnp.bitwise_xor(chip, 2 * kv + i)
-            o_own_ref[target] = out[i * ROWS : (i + 1) * ROWS]
-            o_other_ref[target] = out[(2 + i) * ROWS : (3 + i) * ROWS]
-        lse = m_ref[kv] * SCALE2 + jnp.log2(den)
+            o_own_ref[target, here, :] = out[i * ROWS : (i + 1) * ROWS]
+            o_other_ref[target, here, :] = out[(2 + i) * ROWS : (3 + i) * ROWS]
+        lse = m_ref[u % 4] * SCALE2 + jnp.log2(den)
         for side in range(2):
             block = lse[side * HD : (side + 1) * HD]
             line = jnp.sum(jnp.where(rows == lanes, block, 0.0), axis=0, keepdims=True)
             line = jnp.where(odd == 1, pltpu.roll(line, ROWS, 1), line)
-            lse_ref[0, pl.ds(side * KVH + head(kv), 1), :] = line
-
-    def whole(masked):
-        for stage in range(KVH + 2):
+            lse_ref[sub, pl.ds(side * KVH + head(kv), 1), :] = line
+
+    def whole(units, live):
+        count = len(units)
+        for stage in range(count + 2):
             top = None
-            q = query(stage) if stage < KVH else None
+            q = query(*units[stage]) if stage < count else None
             if stage > 1:
-                value(stage - 2)
+                value(stage - 2, *units[stage - 2])
             for i in range(tiles):
-                if stage < KVH:
-                    top = score(stage, i, q, top, masked)
-                if 0 < stage <= KVH:
+                if stage < count:
+                    top = score(stage, *units[stage], i, q, top, live)
+                if 0 < stage <= count:
                     soft(stage - 1, i)
-            if stage < KVH:
+            if stage < count:
                 close(stage, top)
 
-    @pl.when(live <= 0)
+    full = living(0) >= span
+    for sub in range(1, TOGETHER):
+        full = jnp.logical_and(full, living(sub) >= span)
+
+    @pl.when(full)
     def _():
-        o_own_ref[...] = jnp.zeros(o_own_ref.shape, BF16)
-        o_other_ref[...] = jnp.zeros(o_other_ref.shape, BF16)
-        lse_ref[...] = jnp.full(lse_ref.shape, DEAD, F32)
-
-    @pl.when(live >= span)
+        whole([(sub, kv) for sub in range(TOGETHER) for kv in range(KVH)], None)
+
+    @pl.when(jnp.logical_not(full))
     def _():
-        whole(False)
-
-    @pl.when(jnp.logical_and(live > 0, live < span))
-    def _():
-        whole(True)
+        @pl.loop(0, TOGETHER)
+        def _(sub):
+            live = living(sub)
+
+            @pl.when(live <= 0)
+            def _():
+                here = pl.ds(pl.multiple_of(sub * ROWS, ROWS), ROWS)
+                blank = jnp.zeros((ROWS, HD), BF16)
+                for c in range(CHIPS):
+                    o_own_ref[c, here, :] = blank
+                    o_other_ref[c, here, :] = blank
+                lse_ref[sub] = jnp.full((2 * KVH, HD), DEAD, F32)
+
+            @pl.when(live > 0)
+            def _():
+                whole([(sub, kv) for kv in range(KVH)], live)
 
 
 def join_kernel(mine_ref, theirs_ref, lse_ref, lse_in_ref, out_ref):
@@ -450,8 +468,8 @@
     q_other += [swap(x) for x in q_own[6:]]
     kv_own = exchange(keyval, "chip")
 
-    o_spec = pl.BlockSpec((CHIPS, ROWS, HD), lambda b: (0, b, 0))
-    kv_spec = pl.BlockSpec((1, span, KVH * HD), lambda b: (b, 0, 0))
+    o_spec = pl.BlockSpec((CHIPS, TOGETHER * ROWS, HD), lambda b: (0, b, 0))
+    kv_spec = pl.BlockSpec((TOGETHER, span, KVH * HD), lambda b: (b, 0, 0))
     attend = pl.pallas_call(
         attend_kernel,
         cost_estimate=pl.CostEstimate(
@@ -459,7 +477,7 @@
             bytes_accessed=4 * WIDE * span * KVH * HD,
             transcendentals=WIDE * KVH * KVH * ROWS * span,
         ),
-        compiler_params=pltpu.CompilerParams(vmem_limit_bytes=16 * 1024 * 1024),
+        compiler_params=pltpu.CompilerParams(vmem_limit_bytes=18 * 1024 * 1024),
         scratch_shapes=[
             pltpu.VMEM((2, KVH * ROWS, span), F32),
             pltpu.VMEM((2, KVH * ROWS, span), BF16),
@@ -470,9 +488,9 @@
             shape((CHIPS, WIDE * ROWS, HD), BF16),
             shape((WIDE, 2 * KVH, HD), F32),
         ),
-        grid=(WIDE,),
+        grid=(WIDE // TOGETHER,),
         in_specs=[smem()] + [vmem()] * (CHIPS * CORES) + [kv_spec] * 2,
-        out_specs=(o_spec, o_spec, pl.BlockSpec((1, 2 * KVH, HD), lambda b: (b, 0, 0))),
+        out_specs=(o_spec, o_spec, pl.BlockSpec((TOGETHER, 2 * KVH, HD), lambda b: (b, 0, 0))),
     )
     o_own, o_other, lse = attend(
         cache_lengths, *q_own, *q_other, far(cache_keys), far(cache_values)

time: 134 us -> 133 us (level)
  no operation moved by 1% of the time
where the time goes in v2:
time: 133 us
  blocking collectives  43 us (32%)
  waiting for transfers between devices  38.2 us (29%)
  Pallas kernels  32.1 us (24%)
  starting transfers between devices  18.8 us (14%)
    all_to_all x2, blocking collectives, exchange(): return lax.all_to_all(x, axes, split_axis=0, concat_axis=0, tiled=True)  43 us
    all_to_all x2, waiting for transfers between devices, exchange(): return lax.all_to_all(x, axes, split_axis=0, concat_axis=0, tiled=True)  19.8 us
    pallas_call x1, Pallas kernels, local(): attend(cache_lengths, *q_own, *q_other, far(cache_keys), far(cache_values))  16 us
    ppermute x7, waiting for transfers between devices, hop(): return lax.ppermute(x, 'chip', [(c, c ^ distance) for c in range(CHIPS)])  10.2 us
    ppermute x7, starting transfers between devices, hop(): return lax.ppermute(x, 'chip', [(c, c ^ distance) for c in range(CHIPS)])  8.98 us
    ppermute x13, waiting for transfers between devices, swap(): return lax.ppermute(x, 'core', [(0, 1), (1, 0)])  8.23 us
    all_to_all x2, starting transfers between devices, exchange(): return lax.all_to_all(x, axes, split_axis=0, concat_axis=0, tiled=True)  7.7 us
    pallas_call x1, Pallas kernels, local(): pl.pallas_call(draft_kernel, compiler_params=pltpu.CompilerParams(vmem_li...  3.33 us
  transfers between devices with their start and end apart: 22, of which 13 were waited for; matrix products, arithmetic and copies ran while one was open for 0% of the time, Pallas kernels for 6%

profile of v2, /device:TPU:0, one launch (start us, length us, event | category | flops | bytes accessed | tf_op | source)
XLA Modules:
  0.0 133.0 jit_solution(353604584212767038)
XLA Ops:
  0.0 0.0 copy-start.1
  0.0 1.0 shard_map.118
  1.0 25.6 %all_to_all.20 = bf16[64,40,128]{2,1,0:T(8,128)(2,1)S(1)} all-to-all(bf16[64,40,128]{2,1,0:T(8,128)(2,1)S(1)} %bitcast.9), channel_id=1, replica_groups=mesh['wide'=8,'chip'=8,'core'=2] {'wide','chip'}, dimensions={0} | all-to-all | bytes 1310720 | tf_op jit(solution)/shard_map/all_to_all | solution.py:395
  26.6 0.0 collective-permute-start
  26.6 2.1 %collective-permute-done = bf16[64,40,128]{2,1,0:T(8,128)(2,1)S(1)} collective-permute-done((bf16[64,40,128]{2,1,0:T(8,128)(2,1)S(1)}, bf16[64,40,128]{2,1,0:T(8,128)(2,1)S(1)}, u32[]{:S(2)}, u32[]{:S(2)}) %collective-permute-start) | collective-permute-done | bytes 655392 | tf_op jit(solution)/shard_map/ppermute | solution.py:387
  28.7 2.7 %shard_map.119 = (bf16[512,128]{1,0:T(8,128)(2,1)S(1)}, bf16[128,256]{1,0:T(8,128)(2,1)S(1)}, bf16[8,8,128]{2,1,0:T(8,128)(2,1)S(1)}) custom-call(bf16[8,8,40,128]{3,2,1,0:T(8,128)(2,1)S(1)} %bitcast.10, bf16[8,8,40,128]{3,2,1,0:T(8,128)(2,1)S(1)} %bitcast.13, f32[32,128]{1,0:T(8,128)} %bitcast.16, bf16[8,2,256,512]{3,2,1,0:T(8,128)(2,1)} %bitcast.15, ...), custom_call_target="tpu_custom_call" | custom-call | tf_op jit(solution)/shard_map/pallas_call | solution.py:430
  31.4 1.8 %collective-permute-start.4 = (bf16[512,128]{1,0:T(8,128)(2,1)S(1)}, bf16[512,128]{1,0:T(8,128)(2,1)S(1)}, u32[]{:S(2)}, u32[]{:S(2)}) collective-permute-start(bf16[512,128]{1,0:T(8,128)(2,1)S(1)} %get-tuple-element.15.refs_0_.q_ref), channel_id=1, source_target_pairs={{0,8},{2,10},{4,12},{6,14},{8,0},{10,2},{12,4},{14,6},{1,9},{3,11}... | collective-permute-start | bytes 393224 | tf_op jit(solution)/shard_map/ppermute | solution.py:391
  33.2 0.0 collective-permute-start.8
  33.2 1.2 collective-permute-start.3
  34.3 1.5 %collective-permute-start.2 = (bf16[512,128]{1,0:T(8,128)(2,1)S(1)}, bf16[512,128]{1,0:T(8,128)(2,1)S(1)}, u32[]{:S(2)}, u32[]{:S(2)}) collective-permute-start(bf16[512,128]{1,0:T(8,128)(2,1)S(1)} %get-tuple-element.15.refs_0_.q_ref), channel_id=1, source_target_pairs={{0,4},{2,6},{4,0},{6,2},{8,12},{10,14},{12,8},{14,10},{1,5},{3,7},... | collective-permute-start | bytes 393224 | tf_op jit(solution)/shard_map/ppermute | solution.py:391
  35.8 1.5 %collective-permute-start.1 = (bf16[512,128]{1,0:T(8,128)(2,1)S(1)}, bf16[512,128]{1,0:T(8,128)(2,1)S(1)}, u32[]{:S(2)}, u32[]{:S(2)}) collective-permute-start(bf16[512,128]{1,0:T(8,128)(2,1)S(1)} %get-tuple-element.15.refs_0_.q_ref), channel_id=1, source_target_pairs={{0,2},{2,0},{4,6},{6,4},{8,10},{10,8},{12,14},{14,12},{1,3},{3,1},... | collective-permute-start | bytes 393224 | tf_op jit(solution)/shard_map/ppermute | solution.py:391
  37.3 1.2 collective-permute-done.4.refs_4_
  38.5 0.0 collective-permute-start.12
  38.5 0.0 collective-permute-done.8.refs_8_
  38.5 1.4 %collective-permute-start.7 = (bf16[512,128]{1,0:T(8,128)(2,1)S(1)}, bf16[512,128]{1,0:T(8,128)(2,1)S(1)}, u32[]{:S(2)}, u32[]{:S(2)}) collective-permute-start(bf16[512,128]{1,0:T(8,128)(2,1)S(1)} %collective-permute-done.4.refs_4_), channel_id=1, source_target_pairs={{0,6},{2,4},{4,2},{6,0},{8,14},{10,12},{12,10},{14,8},{1,7},{3,5},... | collective-permute-start | bytes 393224 | tf_op jit(solution)/shard_map/ppermute | solution.py:391
  39.9 3.4 %collective-permute-done.3.refs_3_ = bf16[512,128]{1,0:T(8,128)(2,1)S(1)} collective-permute-done((bf16[512,128]{1,0:T(8,128)(2,1)S(1)}, bf16[512,128]{1,0:T(8,128)(2,1)S(1)}, u32[]{:S(2)}, u32[]{:S(2)}) %collective-permute-start.3) | collective-permute-done | bytes 131104 | tf_op jit(solution)/shard_map/ppermute | solution.py:391
  43.4 0.0 collective-permute-start.6
  43.4 0.0 collective-permute-done.2.refs_2_
  43.4 1.7 %collective-permute-start.5 = (bf16[512,128]{1,0:T(8,128)(2,1)S(1)}, bf16[512,128]{1,0:T(8,128)(2,1)S(1)}, u32[]{:S(2)}, u32[]{:S(2)}) collective-permute-start(bf16[512,128]{1,0:T(8,128)(2,1)S(1)} %collective-permute-done.4.refs_4_), channel_id=1, source_target_pairs={{0,2},{2,0},{4,6},{6,4},{8,10},{10,8},{12,14},{14,12},{1,3},{3,1},... | collective-permute-start | bytes 393224 | tf_op jit(solution)/shard_map/ppermute | solution.py:391
  45.1 0.0 collective-permute-done.1.refs_1_
  45.1 0.0 collective-permute-start.11
  45.1 0.0 collective-permute-done.12.refs_12_
  45.1 0.5 collective-permute-start.10
  45.6 0.3 collective-permute-done.7.refs_7_
  45.9 0.0 collective-permute-start.9
  45.9 5.1 %collective-permute-done.6.refs_6_ = bf16[512,128]{1,0:T(8,128)(2,1)S(1)} collective-permute-done((bf16[512,128]{1,0:T(8,128)(2,1)S(1)}, bf16[512,128]{1,0:T(8,128)(2,1)S(1)}, u32[]{:S(2)}, u32[]{:S(2)}) %collective-permute-start.6) | collective-permute-done | bytes 131104 | tf_op jit(solution)/shard_map/ppermute | solution.py:391
  51.1 0.0 collective-permute-start.15
  51.1 0.0 collective-permute-done.5.refs_5_
  51.1 0.5 collective-permute-start.14
  51.6 0.0 collective-permute-done.11.refs_11_
  51.6 0.1 collective-permute-start.13
  51.7 0.0 collective-permute-done.10.refs_10_
  51.7 0.0 collective-permute-done.9.refs_9_
  51.7 0.7 collective-permute-done.15.refs_15_
  52.4 0.2 collective-permute-done.14.refs_14_
  52.6 0.3 collective-permute-done.13.refs_13_
  52.9 0.0 copy-done.1
  52.9 16.0 %shard_map.120 = (bf16[8,512,128]{2,1,0:T(8,128)(2,1)S(1)}, bf16[8,512,128]{2,1,0:T(8,128)(2,1)S(1)}, f32[8,8,128]{2,1,0:T(8,128)S(1)}) custom-call(s32[8]{0:T(128)S(1)} %copy-done.1, bf16[512,128]{1,0:T(8,128)(2,1)S(1)} %get-tuple-element.15.refs_0_.q_ref, bf16[512,128]{1,0:T(8,128)(2,1)S(1)} %collective-permute-done.1.refs_1_, ...), custom_call_target="tpu_custom_call" | custom-call | flops 8589934592 | bytes 16777216 | tf_op jit(solution)/shard_map/pallas_call | solution.py:495
  69.0 0.0 copy-start.2
  69.0 0.1 collective-permute-start.16
  69.1 2.1 %shard_map.122 = bf16[8,256,128]{2,1,0:T(8,128)(2,1)} custom-call(bf16[128,256]{1,0:T(8,128)(2,1)S(1)} %get-tuple-element.19.slice_ref, bf16[256,1024]{1,0:T(8,128)(2,1)} %wkv_ref.1), custom_call_target="tpu_custom_call" | custom-call | flops 70000000 | bytes 1200000 | tf_op jit(solution)/shard_map/pallas_call | solution.py:453
  71.2 4.1 %all-to-all-start.2 = ((bf16[8,256,128]{2,1,0:T(8,128)(2,1)}), bf16[8,256,128]{2,1,0:T(8,128)(2,1)}, u32[]{:S(2)}, u32[]{:S(2)}) async-start(bf16[8,256,128]{2,1,0:T(8,128)(2,1)} %shard_map.122), calls=%async_computation.2 | async-start | bytes 1048576 | tf_op jit(solution)/shard_map/all_to_all | solution.py:395
  75.3 0.8 collective-permute-start.17
  76.1 0.9 collective-permute-done.17.lse_in_ref
  76.9 0.0 collective-permute-done.16.theirs_ref
  76.9 2.5 %shard_map.121 = bf16[8,528,128]{2,1,0:T(8,128)(2,1)} custom-call(bf16[8,512,128]{2,1,0:T(8,128)(2,1)S(1)} %get-tuple-element.16.mine_ref, bf16[8,512,128]{2,1,0:T(8,128)(2,1)S(1)} %collective-permute-done.16.theirs_ref, f32[8,8,128]{2,1,0:T(8,128)S(1)} %get-tuple-element.18.lse_ref, f32[8,8,128]{2,1,0:T(8,128)S(1)} %collective-permute-done.17.lse_in_ref), custom_call_target="tpu_custom_call" | custom-call | tf_op jit(solution)/shard_map/pallas_call | solution.py:500
  79.4 8.4 %all-to-all-done.2.kv_own_ref = bf16[8,256,128]{2,1,0:T(8,128)(2,1)} async-done(((bf16[8,256,128]{2,1,0:T(8,128)(2,1)}), bf16[8,256,128]{2,1,0:T(8,128)(2,1)}, u32[]{:S(2)}, u32[]{:S(2)}) %all-to-all-start.2) | async-done | bytes 524320 | tf_op jit(solution)/shard_map/all_to_all | solution.py:395
  87.8 3.6 %all-to-all-start.1 = ((bf16[8,528,128]{2,1,0:T(8,128)(2,1)}), bf16[8,528,128]{2,1,0:T(8,128)(2,1)S(1)}, u32[]{:S(2)}, u32[]{:S(2)}) async-start(bf16[8,528,128]{2,1,0:T(8,128)(2,1)} %shard_map.121), calls=%async_computation.1 | async-start | bytes 2162688 | tf_op jit(solution)/shard_map/all_to_all | solution.py:395
  91.4 0.1 collective-permute-start.18
  91.5 2.1 %collective-permute-done.18.kv_other_ref = bf16[8,256,128]{2,1,0:T(8,128)(2,1)S(1)} collective-permute-done((bf16[8,256,128]{2,1,0:T(8,128)(2,1)}, bf16[8,256,128]{2,1,0:T(8,128)(2,1)S(1)}, u32[]{:S(2)}, u32[]{:S(2)}) %collective-permute-start.18) | collective-permute-done | bytes 524320 | tf_op jit(solution)/shard_map/ppermute | solution.py:387
  93.6 0.0 copy-start.3
  93.6 0.8 copy-done.3
  94.4 0.0 copy-done.2
  94.4 3.3 %shard_map.123 = (f32[512,128]{1,0:T(8,128)S(1)}, f32[512,128]{1,0:T(8,128)S(1)}) custom-call(bf16[512,128]{1,0:T(8,128)(2,1)S(1)} %get-tuple-element.15.refs_0_.q_ref, bf16[8,256,128]{2,1,0:T(8,128)(2,1)} %all-to-all-done.2.kv_own_ref, bf16[8,256,128]{2,1,0:T(8,128)(2,1)} %copy-done.3, f32[1,128]{1,0:T(1,128)S(1)} %bitcast.14, ...), custom_call_target="tpu_custom_call" | custom-call | flops 4000000000 | bytes 2000000 | tf_op jit(solution)/shard_map/pallas_call | solution.py:509
  97.7 11.3 %all-to-all-done.1.part_ref = bf16[8,528,128]{2,1,0:T(8,128)(2,1)S(1)} async-done(((bf16[8,528,128]{2,1,0:T(8,128)(2,1)}), bf16[8,528,128]{2,1,0:T(8,128)(2,1)S(1)}, u32[]{:S(2)}, u32[]{:S(2)}) %all-to-all-start.1) | async-done | bytes 1081376 | tf_op jit(solution)/shard_map/all_to_all | solution.py:395
  109.1 0.0 copy-start
  109.1 3.1 %shard_map.124 = (bf16[8,8,16,256]{3,2,1,0:T(8,128)(2,1)S(1)}, bf16[8,8,16,256]{3,2,1,0:T(8,128)(2,1)S(1)}) custom-call(bf16[8,528,128]{2,1,0:T(8,128)(2,1)S(1)} %all-to-all-done.1.part_ref, f32[512,128]{1,0:T(8,128)S(1)} %get-tuple-element.21.draft_ref, f32[512,128]{1,0:T(8,128)S(1)} %get-tuple-element.22.lse_ref, bf16[512,4096]{1,0:T(8,128)(2,1)} %wo_far.1), custom_call_target="tpu_custom_call" | custom-call | tf_op jit(solution)/shard_map/pallas_call | solution.py:520
  112.2 0.1 collective-permute-start.19
  112.3 1.9 %collective-permute-done.19.two_ref = bf16[8,8,16,256]{3,2,1,0:T(8,128)(2,1)S(1)} collective-permute-done((bf16[8,8,16,256]{3,2,1,0:T(8,128)(2,1)S(1)}, bf16[8,8,16,256]{3,2,1,0:T(8,128)(2,1)S(1)}, u32[]{:S(2)}, u32[]{:S(2)}) %collective-permute-start.19) | collective-permute-done | bytes 524320 | tf_op jit(solution)/shard_map/ppermute | solution.py:387
  114.2 0.1 shard_map.125
  114.3 17.5 %all_to_all.21 = bf16[64,16,256]{2,1,0:T(8,128)(2,1)S(1)} all-to-all(bf16[64,16,256]{2,1,0:T(8,128)(2,1)S(1)} %bitcast.11), channel_id=1, replica_groups=mesh['wide'=8,'chip'=8,'core'=2] {'wide','chip'}, dimensions={0} | all-to-all | bytes 1048576 | tf_op jit(solution)/shard_map/all_to_all | solution.py:395
  131.7 0.0 copy-done
  131.7 1.2 shard_map.126
Async XLA Ops:
  0.0 52.9 %copy-start.1 = (s32[8]{0:T(128)S(1)}, s32[8]{0:T(128)}, u32[]{:S(2)}) copy-start(s32[8]{0:T(128)} %length_ref.1) | copy-start | bytes 100
  26.6 2.1 %collective-permute-start = (bf16[64,40,128]{2,1,0:T(8,128)(2,1)S(1)}, bf16[64,40,128]{2,1,0:T(8,128)(2,1)S(1)}, u32[]{:S(2)}, u32[]{:S(2)}) collective-permute-start(bf16[64,40,128]{2,1,0:T(8,128)(2,1)S(1)} %all_to_all.20), channel_id=1, source_target_pairs={{0,1},{1,0},{2,3},{3,2},{4,5},{5,4},{6,7},{7,6},{8,9},{9,8},{10,11... | collective-permute-start | bytes 1966088 | tf_op jit(solution)/shard_map/ppermute | solution.py:387
  31.4 7.1 %collective-permute-start.4 = (bf16[512,128]{1,0:T(8,128)(2,1)S(1)}, bf16[512,128]{1,0:T(8,128)(2,1)S(1)}, u32[]{:S(2)}, u32[]{:S(2)}) collective-permute-start(bf16[512,128]{1,0:T(8,128)(2,1)S(1)} %get-tuple-element.15.refs_0_.q_ref), channel_id=1, source_target_pairs={{0,8},{2,10},{4,12},{6,14},{8,0},{10,2},{12,4},{14,6},{1,9},{3,11}... | collective-permute-start | bytes 393224 | tf_op jit(solution)/shard_map/ppermute | solution.py:391
  33.2 5.4 %collective-permute-start.8 = (bf16[512,128]{1,0:T(8,128)(2,1)S(1)}, bf16[512,128]{1,0:T(8,128)(2,1)S(1)}, u32[]{:S(2)}, u32[]{:S(2)}) collective-permute-start(bf16[512,128]{1,0:T(8,128)(2,1)S(1)} %get-tuple-element.15.refs_0_.q_ref), channel_id=1, source_target_pairs={{0,1},{1,0},{2,3},{3,2},{4,5},{5,4},{6,7},{7,6},{8,9},{9,8},{10,11... | collective-permute-start | bytes 393224 | tf_op jit(solution)/shard_map/ppermute | solution.py:387
  33.2 10.2 %collective-permute-start.3 = (bf16[512,128]{1,0:T(8,128)(2,1)S(1)}, bf16[512,128]{1,0:T(8,128)(2,1)S(1)}, u32[]{:S(2)}, u32[]{:S(2)}) collective-permute-start(bf16[512,128]{1,0:T(8,128)(2,1)S(1)} %get-tuple-element.15.refs_0_.q_ref), channel_id=1, source_target_pairs={{0,6},{2,4},{4,2},{6,0},{8,14},{10,12},{12,10},{14,8},{1,7},{3,5},... | collective-permute-start | bytes 393224 | tf_op jit(solution)/shard_map/ppermute | solution.py:391
  34.3 9.0 %collective-permute-start.2 = (bf16[512,128]{1,0:T(8,128)(2,1)S(1)}, bf16[512,128]{1,0:T(8,128)(2,1)S(1)}, u32[]{:S(2)}, u32[]{:S(2)}) collective-permute-start(bf16[512,128]{1,0:T(8,128)(2,1)S(1)} %get-tuple-element.15.refs_0_.q_ref), channel_id=1, source_target_pairs={{0,4},{2,6},{4,0},{6,2},{8,12},{10,14},{12,8},{14,10},{1,5},{3,7},... | collective-permute-start | bytes 393224 | tf_op jit(solution)/shard_map/ppermute | solution.py:391
  35.8 9.3 %collective-permute-start.1 = (bf16[512,128]{1,0:T(8,128)(2,1)S(1)}, bf16[512,128]{1,0:T(8,128)(2,1)S(1)}, u32[]{:S(2)}, u32[]{:S(2)}) collective-permute-start(bf16[512,128]{1,0:T(8,128)(2,1)S(1)} %get-tuple-element.15.refs_0_.q_ref), channel_id=1, source_target_pairs={{0,2},{2,0},{4,6},{6,4},{8,10},{10,8},{12,14},{14,12},{1,3},{3,1},... | collective-permute-start | bytes 393224 | tf_op jit(solution)/shard_map/ppermute | solution.py:391
  38.5 6.6 %collective-permute-start.12 = (bf16[512,128]{1,0:T(8,128)(2,1)S(1)}, bf16[512,128]{1,0:T(8,128)(2,1)S(1)}, u32[]{:S(2)}, u32[]{:S(2)}) collective-permute-start(bf16[512,128]{1,0:T(8,128)(2,1)S(1)} %collective-permute-done.4.refs_4_), channel_id=1, source_target_pairs={{0,1},{1,0},{2,3},{3,2},{4,5},{5,4},{6,7},{7,6},{8,9},{9,8},{10,11... | collective-permute-start | bytes 393224 | tf_op jit(solution)/shard_map/ppermute | solution.py:387
  38.5 7.4 %collective-permute-start.7 = (bf16[512,128]{1,0:T(8,128)(2,1)S(1)}, bf16[512,128]{1,0:T(8,128)(2,1)S(1)}, u32[]{:S(2)}, u32[]{:S(2)}) collective-permute-start(bf16[512,128]{1,0:T(8,128)(2,1)S(1)} %collective-permute-done.4.refs_4_), channel_id=1, source_target_pairs={{0,6},{2,4},{4,2},{6,0},{8,14},{10,12},{12,10},{14,8},{1,7},{3,5},... | collective-permute-start | bytes 393224 | tf_op jit(solution)/shard_map/ppermute | solution.py:391
  43.4 7.7 %collective-permute-start.6 = (bf16[512,128]{1,0:T(8,128)(2,1)S(1)}, bf16[512,128]{1,0:T(8,128)(2,1)S(1)}, u32[]{:S(2)}, u32[]{:S(2)}) collective-permute-start(bf16[512,128]{1,0:T(8,128)(2,1)S(1)} %collective-permute-done.4.refs_4_), channel_id=1, source_target_pairs={{0,4},{2,6},{4,0},{6,2},{8,12},{10,14},{12,8},{14,10},{1,5},{3,7},... | collective-permute-start | bytes 393224 | tf_op jit(solution)/shard_map/ppermute | solution.py:391
  43.4 7.7 %collective-permute-start.5 = (bf16[512,128]{1,0:T(8,128)(2,1)S(1)}, bf16[512,128]{1,0:T(8,128)(2,1)S(1)}, u32[]{:S(2)}, u32[]{:S(2)}) collective-permute-start(bf16[512,128]{1,0:T(8,128)(2,1)S(1)} %collective-permute-done.4.refs_4_), channel_id=1, source_target_pairs={{0,2},{2,0},{4,6},{6,4},{8,10},{10,8},{12,14},{14,12},{1,3},{3,1},... | collective-permute-start | bytes 393224 | tf_op jit(solution)/shard_map/ppermute | solution.py:391
  45.1 6.5 %collective-permute-start.11 = (bf16[512,128]{1,0:T(8,128)(2,1)S(1)}, bf16[512,128]{1,0:T(8,128)(2,1)S(1)}, u32[]{:S(2)}, u32[]{:S(2)}) collective-permute-start(bf16[512,128]{1,0:T(8,128)(2,1)S(1)} %collective-permute-done.3.refs_3_), channel_id=1, source_target_pairs={{0,1},{1,0},{2,3},{3,2},{4,5},{5,4},{6,7},{7,6},{8,9},{9,8},{10,11... | collective-permute-start | bytes 393224 | tf_op jit(solution)/shard_map/ppermute | solution.py:387
  45.1 6.6 %collective-permute-start.10 = (bf16[512,128]{1,0:T(8,128)(2,1)S(1)}, bf16[512,128]{1,0:T(8,128)(2,1)S(1)}, u32[]{:S(2)}, u32[]{:S(2)}) collective-permute-start(bf16[512,128]{1,0:T(8,128)(2,1)S(1)} %collective-permute-done.2.refs_2_), channel_id=1, source_target_pairs={{0,1},{1,0},{2,3},{3,2},{4,5},{5,4},{6,7},{7,6},{8,9},{9,8},{10,11... | collective-permute-start | bytes 393224 | tf_op jit(solution)/shard_map/ppermute | solution.py:387
  45.9 5.8 %collective-permute-start.9 = (bf16[512,128]{1,0:T(8,128)(2,1)S(1)}, bf16[512,128]{1,0:T(8,128)(2,1)S(1)}, u32[]{:S(2)}, u32[]{:S(2)}) collective-permute-start(bf16[512,128]{1,0:T(8,128)(2,1)S(1)} %collective-permute-done.1.refs_1_), channel_id=1, source_target_pairs={{0,1},{1,0},{2,3},{3,2},{4,5},{5,4},{6,7},{7,6},{8,9},{9,8},{10,11... | collective-permute-start | bytes 393224 | tf_op jit(solution)/shard_map/ppermute | solution.py:387
  51.1 1.3 %collective-permute-start.15 = (bf16[512,128]{1,0:T(8,128)(2,1)S(1)}, bf16[512,128]{1,0:T(8,128)(2,1)S(1)}, u32[]{:S(2)}, u32[]{:S(2)}) collective-permute-start(bf16[512,128]{1,0:T(8,128)(2,1)S(1)} %collective-permute-done.7.refs_7_), channel_id=1, source_target_pairs={{0,1},{1,0},{2,3},{3,2},{4,5},{5,4},{6,7},{7,6},{8,9},{9,8},{10,11... | collective-permute-start | bytes 393224 | tf_op jit(solution)/shard_map/ppermute | solution.py:387
  51.1 1.5 %collective-permute-start.14 = (bf16[512,128]{1,0:T(8,128)(2,1)S(1)}, bf16[512,128]{1,0:T(8,128)(2,1)S(1)}, u32[]{:S(2)}, u32[]{:S(2)}) collective-permute-start(bf16[512,128]{1,0:T(8,128)(2,1)S(1)} %collective-permute-done.6.refs_6_), channel_id=1, source_target_pairs={{0,1},{1,0},{2,3},{3,2},{4,5},{5,4},{6,7},{7,6},{8,9},{9,8},{10,11... | collective-permute-start | bytes 393224 | tf_op jit(solution)/shard_map/ppermute | solution.py:387
  51.6 1.3 %collective-permute-start.13 = (bf16[512,128]{1,0:T(8,128)(2,1)S(1)}, bf16[512,128]{1,0:T(8,128)(2,1)S(1)}, u32[]{:S(2)}, u32[]{:S(2)}) collective-permute-start(bf16[512,128]{1,0:T(8,128)(2,1)S(1)} %collective-permute-done.5.refs_5_), channel_id=1, source_target_pairs={{0,1},{1,0},{2,3},{3,2},{4,5},{5,4},{6,7},{7,6},{8,9},{9,8},{10,11... | collective-permute-start | bytes 393224 | tf_op jit(solution)/shard_map/ppermute | solution.py:387
  69.0 25.4 %copy-start.2 = (f32[128]{0:T(128)S(1)}, f32[128]{0:T(128)}, u32[]{:S(2)}) copy-start(f32[128]{0:T(128)} %param.17) | copy-start | bytes 1540
  69.0 7.9 %collective-permute-start.16 = (bf16[8,512,128]{2,1,0:T(8,128)(2,1)S(1)}, bf16[8,512,128]{2,1,0:T(8,128)(2,1)S(1)}, u32[]{:S(2)}, u32[]{:S(2)}) collective-permute-start(bf16[8,512,128]{2,1,0:T(8,128)(2,1)S(1)} %get-tuple-element.17), channel_id=1, source_target_pairs={{0,1},{1,0},{2,3},{3,2},{4,5},{5,4},{6,7},{7,6},{8,9},{9,8},{10,11... | collective-permute-start | bytes 3145736 | tf_op jit(solution)/shard_map/ppermute | solution.py:387
  71.2 16.7 %all-to-all-start.2 = ((bf16[8,256,128]{2,1,0:T(8,128)(2,1)}), bf16[8,256,128]{2,1,0:T(8,128)(2,1)}, u32[]{:S(2)}, u32[]{:S(2)}) async-start(bf16[8,256,128]{2,1,0:T(8,128)(2,1)} %shard_map.122), calls=%async_computation.2 | async-start | bytes 1048576 | tf_op jit(solution)/shard_map/all_to_all | solution.py:395
  75.3 1.6 %collective-permute-start.17 = (f32[8,8,128]{2,1,0:T(8,128)S(1)}, f32[8,8,128]{2,1,0:T(8,128)S(1)}, u32[]{:S(2)}, u32[]{:S(2)}) collective-permute-start(f32[8,8,128]{2,1,0:T(8,128)S(1)} %get-tuple-element.18.lse_ref), channel_id=1, source_target_pairs={{0,1},{1,0},{2,3},{3,2},{4,5},{5,4},{6,7},{7,6},{8,9},{9,8},{10,11... | collective-permute-start | bytes 98312 | tf_op jit(solution)/shard_map/ppermute | solution.py:387
  87.8 21.2 %all-to-all-start.1 = ((bf16[8,528,128]{2,1,0:T(8,128)(2,1)}), bf16[8,528,128]{2,1,0:T(8,128)(2,1)S(1)}, u32[]{:S(2)}, u32[]{:S(2)}) async-start(bf16[8,528,128]{2,1,0:T(8,128)(2,1)} %shard_map.121), calls=%async_computation.1 | async-start | bytes 2162688 | tf_op jit(solution)/shard_map/all_to_all | solution.py:395
  91.4 2.2 %collective-permute-start.18 = (bf16[8,256,128]{2,1,0:T(8,128)(2,1)}, bf16[8,256,128]{2,1,0:T(8,128)(2,1)S(1)}, u32[]{:S(2)}, u32[]{:S(2)}) collective-permute-start(bf16[8,256,128]{2,1,0:T(8,128)(2,1)} %all-to-all-done.2.kv_own_ref), channel_id=1, source_target_pairs={{0,1},{1,0},{2,3},{3,2},{4,5},{5,4},{6,7},{7,6},{8,9},{9,8},{10,11... | collective-permute-start | bytes 1572872 | tf_op jit(solution)/shard_map/ppermute | solution.py:387
  93.6 0.8 copy-start.3
  109.1 22.7 %copy-start = (s32[8]{0:T(128)S(1)}, s32[8]{0:T(128)}, u32[]{:S(2)}) copy-start(s32[8]{0:T(128)} %owner_ref.3) | copy-start | bytes 100
  112.2 2.0 %collective-permute-start.19 = (bf16[8,8,16,256]{3,2,1,0:T(8,128)(2,1)S(1)}, bf16[8,8,16,256]{3,2,1,0:T(8,128)(2,1)S(1)}, u32[]{:S(2)}, u32[]{:S(2)}) collective-permute-start(bf16[8,8,16,256]{3,2,1,0:T(8,128)(2,1)S(1)} %get-tuple-element.24), channel_id=1, source_target_pairs={{0,1},{1,0},{2,3},{3,2},{4,5},{5,4},{6,7},{7,6},{8,9},{9,8},{10,11... | collective-permute-start | bytes 1572872 | tf_op jit(solution)/shard_map/ppermute | solution.py:387
